TPU v7x, 32 devices: a whole 2x2x4 slice. The times are simulated.
32 devices in a mesh: dp: 4 (over y, core), fsdp: 8 (over z, x).
Axes of the slice: x: 2, y: 2, z: 4, core: 2. Of those that a mesh axis runs over, the one named last changes fastest.
Arguments:
- words: bfloat16 [128, 20, 768], P(('dp', 'fsdp')), may hold values from -6 to 6
- regions: bfloat16 [128, 36, 768], P(('dp', 'fsdp')), may hold values from -6 to 6
- word_count: int32 [128], P(('dp', 'fsdp')), may hold values from 5 to 20, as said below
- region_count: int32 [128], P(('dp', 'fsdp')), may hold values from 10 to 36, as said below
- attn_qkv: bfloat16 [3, 3, 768, 768], P(None, None, 'fsdp'), may hold values from -0.21875 to 0.21875
- attn_out: bfloat16 [3, 768, 768], P(None, 'fsdp'), may hold values from -0.625 to 0.625
- attn_bias: bfloat16 [3, 3, 768], P(None, None, 'fsdp'), may hold values from -3 to 3
- ffn_in: bfloat16 [2, 768, 3072], P(None, 'fsdp'), may hold values from -0.21875 to 0.21875
- ffn_in_bias: bfloat16 [2, 3072], P(None, 'fsdp'), may hold values from -3 to 3
- ffn_out: bfloat16 [2, 3072, 768], P(None, 'fsdp'), may hold values from -0.15625 to 0.15625
- ffn_out_bias: bfloat16 [2, 768], P(None, 'fsdp'), may hold values from -3 to 3
- norm_gain: bfloat16 [5, 768], P(None, 'fsdp'), may hold values from 0.5 to 1.5
- norm_bias: bfloat16 [5, 768], P(None, 'fsdp'), may hold values from -2 to 2
- word_cot: bfloat16 [128, 20, 768], P(('dp', 'fsdp')), may hold values from -6 to 6
- region_cot: bfloat16 [128, 36, 768], P(('dp', 'fsdp')), may hold values from -6 to 6
Outputs:
- lang_out: bfloat16 [128, 20, 768], P(('dp', 'fsdp'))
- vis_out: bfloat16 [128, 36, 768], P(('dp', 'fsdp'))
- words_grad: float32 [128, 20, 768], P(('dp', 'fsdp'))
- regions_grad: float32 [128, 36, 768], P(('dp', 'fsdp'))
- attn_qkv_grad: float32 [3, 3, 768, 768], P(None, None, 'fsdp')
- attn_out_grad: float32 [3, 768, 768], P(None, 'fsdp')
- attn_bias_grad: float32 [3, 3, 768], P(None, None, 'fsdp')
- ffn_in_grad: float32 [2, 768, 3072], P(None, 'fsdp')
- ffn_in_bias_grad: float32 [2, 3072], P(None, 'fsdp')
- ffn_out_grad: float32 [2, 3072, 768], P(None, 'fsdp')
- ffn_out_bias_grad: float32 [2, 768], P(None, 'fsdp')
- norm_gain_grad: float32 [5, 768], P(None, 'fsdp')
- norm_bias_grad: float32 [5, 768], P(None, 'fsdp')
Inputs may be any that keep to these rules, and one draw needn't show every extreme that they name: Each item's first word_count words are live, the rest of its 20 slots are padding. Each item's first region_count regions are live, the rest of its 36 slots are padding.
All inputs are finite; a program needn't handle non-finite values.
Results may differ from a plain program's by a relative error of at most 0.024.
Values may be sent and summed in bfloat16 or wider, within the bound.
A program may use at most 256 MiB of HBM per device.

v0:
```python
import jax
import jax.numpy as jnp
from jax import lax
from jax.sharding import PartitionSpec as P

HEADS = 12
HEAD_DIM = 64


EPS = 1e-06
NEG = -1e30


def layer_norm(inputs, norm_scale, norm_shift):
    centered = inputs - jnp.mean(inputs, -1, keepdims=True)
    spread = lax.rsqrt(jnp.mean(centered * centered, -1, keepdims=True) + EPS)
    return centered * spread * norm_scale + norm_shift


def norm_core(inputs, norm_scale):
    return layer_norm(inputs, norm_scale, 0.0)


def exact_gelu(inputs):
    return jax.nn.gelu(inputs, approximate=False)


def product(pattern, left, right):
    return jnp.einsum(pattern, left, right, preferred_element_type=jnp.float32)


def split_heads(inputs):
    return inputs.reshape(inputs.shape[0], inputs.shape[1], HEADS, HEAD_DIM)


def three_way(rows_low, weight_three, offsets):
    projected = product("nld,cde->nlce", rows_low, weight_three)
    offset_wide = offsets.astype(jnp.float32)
    queries = split_heads((projected[:, :, 0] + offset_wide[0]).astype(jnp.bfloat16))
    key_rows = split_heads(projected[:, :, 1].astype(jnp.bfloat16))
    value_rows = split_heads((projected[:, :, 2] + offset_wide[1]).astype(jnp.bfloat16))
    return (queries, key_rows, value_rows)


def three_way_back(rows_low, weight_three, query_grad, key_grad, value_grad):
    flat_shape = rows_low.shape
    stacked = jnp.stack(
        [
            query_grad.reshape(flat_shape),
            key_grad.reshape(flat_shape),
            value_grad.reshape(flat_shape),
        ],
        2,
    )
    stacked_low = stacked.astype(jnp.bfloat16)
    rows_grad = product("nlce,cde->nld", stacked_low, weight_three)
    weight_grad = product("nld,nlce->cde", rows_low, stacked_low)
    offset_sums = jnp.sum(stacked, (0, 1))
    return (rows_grad, weight_grad, offset_sums[0], offset_sums[2])


def masked_scores(queries, key_rows, key_live):
    raw_scores = product("nqhe,nkhe->nhqk", queries, key_rows) * HEAD_DIM ** (-0.5)
    return jnp.where(key_live[:, None, None, :], raw_scores, NEG)


def attention_core(queries, key_rows, value_rows, key_live):
    scores = masked_scores(queries, key_rows, key_live)
    top_score = jnp.max(scores, -1, keepdims=True)
    log_total = top_score + jnp.log(jnp.sum(jnp.exp(scores - top_score), -1, keepdims=True))
    weights = jnp.exp(scores - log_total).astype(jnp.bfloat16)
    context = product("nhqk,nkhe->nqhe", weights, value_rows)
    return (context.astype(jnp.bfloat16), log_total)


def attention_back(queries, key_rows, value_rows, key_live, log_total, context_grad):
    probs = jnp.exp(masked_scores(queries, key_rows, key_live) - log_total)
    value_grad = product("nhqk,nqhe->nkhe", probs.astype(jnp.bfloat16), context_grad)
    prob_grad = product("nqhe,nkhe->nhqk", context_grad, value_rows)
    score_grad = (probs * (prob_grad - jnp.sum(probs * prob_grad, -1, keepdims=True))).astype(
        jnp.bfloat16
    )
    scaling = HEAD_DIM ** (-0.5)
    query_grad = product("nhqk,nkhe->nqhe", score_grad, key_rows) * scaling
    key_grad = product("nhqk,nqhe->nkhe", score_grad, queries) * scaling
    return (query_grad, key_grad, value_grad)


def attention_out(stream, context, params):
    flat_context = context.reshape(stream.shape)
    offsets = params[2].astype(jnp.float32)
    summed = (
        stream.astype(jnp.float32) + product("nld,de->nle", flat_context, params[1]) + offsets[2]
    )
    return (
        summed,
        layer_norm(summed, params[3].astype(jnp.float32), params[4].astype(jnp.float32)),
    )


def output_back(summed, context, out_weight, norm_scale, out_grad):
    ignored, pull = jax.vjp(norm_core, summed, norm_scale.astype(jnp.float32))
    summed_grad, scale_grad = pull(out_grad)
    shift_grad = jnp.sum(out_grad, (0, 1))
    flat_grad = summed_grad.astype(jnp.bfloat16)
    out_w_grad = product("nld,nle->de", context.reshape(summed.shape), flat_grad)
    offset_grad = jnp.sum(summed_grad, (0, 1))
    context_grad = split_heads(product("nle,de->nld", flat_grad, out_weight).astype(jnp.bfloat16))
    return (summed_grad, context_grad, out_w_grad, offset_grad, scale_grad, shift_grad)


def self_forward(stream, key_live, params):
    rows_low = stream.astype(jnp.bfloat16)
    parts = three_way(rows_low, params[0], params[2])
    context, log_total = attention_core(parts[0], parts[1], parts[2], key_live)
    summed, result = attention_out(stream, context, params)
    return ((rows_low, parts, context, log_total, summed), result)


def self_back(kept, key_live, back_params, out_grad):
    rows_low, parts, context, log_total, summed = kept
    summed_grad, context_grad, out_w_grad, out_off_grad, scale_grad, shift_grad = output_back(
        summed, context, back_params[1], back_params[2], out_grad
    )
    query_grad, key_grad, value_grad = attention_back(
        parts[0], parts[1], parts[2], key_live, log_total, context_grad
    )
    rows_grad, weight_grad, query_off, value_off = three_way_back(
        rows_low, back_params[0], query_grad, key_grad, value_grad
    )
    grads = (
        weight_grad,
        out_w_grad,
        jnp.stack([query_off, value_off, out_off_grad]),
        scale_grad,
        shift_grad,
    )
    return (summed_grad + rows_grad, grads)


def ffn_forward(stream, params):
    rows_low = stream.astype(jnp.bfloat16)
    pre_act = product("nld,df->nlf", rows_low, params[0]) + params[1].astype(jnp.float32)
    activated, gelu_pull = jax.vjp(exact_gelu, pre_act)
    act_low = activated.astype(jnp.bfloat16)
    summed = stream + product("nlf,fd->nld", act_low, params[2]) + params[3].astype(jnp.float32)
    result = layer_norm(summed, params[4].astype(jnp.float32), params[5].astype(jnp.float32))
    return ((rows_low, act_low, gelu_pull, summed), result)


def ffn_back(kept, back_params, out_grad):
    rows_low, act_low, gelu_pull, summed = kept
    ignored, pull = jax.vjp(norm_core, summed, back_params[2].astype(jnp.float32))
    summed_grad, scale_grad = pull(out_grad)
    flat_grad = summed_grad.astype(jnp.bfloat16)
    out_w_grad = product("nlf,nld->fd", act_low, flat_grad)
    act_grad = product("nld,fd->nlf", flat_grad, back_params[1])
    (pre_grad,) = gelu_pull(act_grad)
    pre_low = pre_grad.astype(jnp.bfloat16)
    in_w_grad = product("nld,nlf->df", rows_low, pre_low)
    rows_grad = summed_grad + product("nlf,df->nld", pre_low, back_params[0])
    grads = (
        in_w_grad,
        jnp.sum(pre_grad, (0, 1)),
        out_w_grad,
        jnp.sum(summed_grad, (0, 1)),
        scale_grad,
        jnp.sum(out_grad, (0, 1)),
    )
    return (rows_grad, grads)


def local(
    words,
    regions,
    word_count,
    region_count,
    attn_qkv,
    attn_out,
    attn_bias,
    ffn_in,
    ffn_in_bias,
    ffn_out,
    ffn_out_bias,
    norm_gain,
    norm_bias,
    word_cot,
    region_cot,
):
    word_live = jnp.arange(words.shape[1], dtype=jnp.int32)[None, :] < word_count[:, None]
    region_live = jnp.arange(regions.shape[1], dtype=jnp.int32)[None, :] < region_count[:, None]

    def attention_params(module):
        return (
            lax.all_gather(attn_qkv[module], "fsdp", axis=1, tiled=True),
            lax.all_gather(attn_out[module], "fsdp", axis=0, tiled=True),
            lax.all_gather(attn_bias[module], "fsdp", axis=1, tiled=True),
            lax.all_gather(norm_gain[module], "fsdp", axis=0, tiled=True),
            lax.all_gather(norm_bias[module], "fsdp", axis=0, tiled=True),
        )

    def attention_params_again(module):
        return (
            lax.all_gather(attn_qkv[module], "fsdp", axis=1, tiled=True),
            lax.all_gather(attn_out[module], "fsdp", axis=0, tiled=True),
            lax.all_gather(norm_gain[module], "fsdp", axis=0, tiled=True),
        )

    def ffn_params(stream):
        return (
            lax.all_gather(ffn_in[stream], "fsdp", axis=0, tiled=True),
            lax.all_gather(ffn_in_bias[stream], "fsdp", axis=0, tiled=True),
            lax.all_gather(ffn_out[stream], "fsdp", axis=0, tiled=True),
            lax.all_gather(ffn_out_bias[stream], "fsdp", axis=0, tiled=True),
            lax.all_gather(norm_gain[3 + stream], "fsdp", axis=0, tiled=True),
            lax.all_gather(norm_bias[3 + stream], "fsdp", axis=0, tiled=True),
        )

    def ffn_params_again(stream):
        return (
            lax.all_gather(ffn_in[stream], "fsdp", axis=0, tiled=True),
            lax.all_gather(ffn_out[stream], "fsdp", axis=0, tiled=True),
            lax.all_gather(norm_gain[3 + stream], "fsdp", axis=0, tiled=True),
        )

    def reduce_attention(grads):
        shards = (
            lax.psum_scatter(
                grads[0].astype(jnp.bfloat16), "fsdp", scatter_dimension=1, tiled=True
            ).astype(jnp.float32),
            lax.psum_scatter(
                grads[1].astype(jnp.bfloat16), "fsdp", scatter_dimension=0, tiled=True
            ).astype(jnp.float32),
            lax.psum_scatter(
                grads[2].astype(jnp.bfloat16), "fsdp", scatter_dimension=1, tiled=True
            ).astype(jnp.float32),
            lax.psum_scatter(
                grads[3].astype(jnp.bfloat16), "fsdp", scatter_dimension=0, tiled=True
            ).astype(jnp.float32),
            lax.psum_scatter(
                grads[4].astype(jnp.bfloat16), "fsdp", scatter_dimension=0, tiled=True
            ).astype(jnp.float32),
        )
        return (
            lax.psum(shards[0].astype(jnp.bfloat16), "dp").astype(jnp.float32),
            lax.psum(shards[1].astype(jnp.bfloat16), "dp").astype(jnp.float32),
            lax.psum(shards[2].astype(jnp.bfloat16), "dp").astype(jnp.float32),
            lax.psum(shards[3].astype(jnp.bfloat16), "dp").astype(jnp.float32),
            lax.psum(shards[4].astype(jnp.bfloat16), "dp").astype(jnp.float32),
        )

    def reduce_ffn(grads):
        shards = (
            lax.psum_scatter(
                grads[0].astype(jnp.bfloat16), "fsdp", scatter_dimension=0, tiled=True
            ).astype(jnp.float32),
            lax.psum_scatter(
                grads[1].astype(jnp.bfloat16), "fsdp", scatter_dimension=0, tiled=True
            ).astype(jnp.float32),
            lax.psum_scatter(
                grads[2].astype(jnp.bfloat16), "fsdp", scatter_dimension=0, tiled=True
            ).astype(jnp.float32),
            lax.psum_scatter(
                grads[3].astype(jnp.bfloat16), "fsdp", scatter_dimension=0, tiled=True
            ).astype(jnp.float32),
            lax.psum_scatter(
                grads[4].astype(jnp.bfloat16), "fsdp", scatter_dimension=0, tiled=True
            ).astype(jnp.float32),
            lax.psum_scatter(
                grads[5].astype(jnp.bfloat16), "fsdp", scatter_dimension=0, tiled=True
            ).astype(jnp.float32),
        )
        return (
            lax.psum(shards[0].astype(jnp.bfloat16), "dp").astype(jnp.float32),
            lax.psum(shards[1].astype(jnp.bfloat16), "dp").astype(jnp.float32),
            lax.psum(shards[2].astype(jnp.bfloat16), "dp").astype(jnp.float32),
            lax.psum(shards[3].astype(jnp.bfloat16), "dp").astype(jnp.float32),
            lax.psum(shards[4].astype(jnp.bfloat16), "dp").astype(jnp.float32),
            lax.psum(shards[5].astype(jnp.bfloat16), "dp").astype(jnp.float32),
        )

    cross = attention_params(0)
    lang_parts = three_way(words, cross[0], cross[2])
    vis_parts = three_way(regions, cross[0], cross[2])
    lang_context, lang_total = attention_core(
        lang_parts[0], vis_parts[1], vis_parts[2], region_live
    )
    vis_context, vis_total = attention_core(vis_parts[0], lang_parts[1], lang_parts[2], word_live)
    lang_cross_sum, lang_one = attention_out(words, lang_context, cross)
    vis_cross_sum, vis_one = attention_out(regions, vis_context, cross)
    lang_self = attention_params(1)
    lang_self_kept, lang_two = self_forward(lang_one, word_live, lang_self)
    vis_self = attention_params(2)
    vis_self_kept, vis_two = self_forward(vis_one, region_live, vis_self)
    lang_ffn = ffn_params(0)
    lang_ffn_kept, lang_three = ffn_forward(lang_two, lang_ffn)
    vis_ffn = ffn_params(1)
    vis_ffn_kept, vis_three = ffn_forward(vis_two, vis_ffn)
    lang_grad = jnp.where(word_live[:, :, None], word_cot.astype(jnp.float32), 0.0)
    vis_grad = jnp.where(region_live[:, :, None], region_cot.astype(jnp.float32), 0.0)
    lang_ffn_back = ffn_params_again(0)
    lang_grad, lang_ffn_grads = ffn_back(lang_ffn_kept, lang_ffn_back, lang_grad)
    lang_ffn_grads = reduce_ffn(lang_ffn_grads)
    vis_ffn_back = ffn_params_again(1)
    vis_grad, vis_ffn_grads = ffn_back(vis_ffn_kept, vis_ffn_back, vis_grad)
    vis_ffn_grads = reduce_ffn(vis_ffn_grads)
    lang_self_back = attention_params_again(1)
    lang_grad, lang_self_grads = self_back(lang_self_kept, word_live, lang_self_back, lang_grad)
    lang_self_grads = reduce_attention(lang_self_grads)
    vis_self_back = attention_params_again(2)
    vis_grad, vis_self_grads = self_back(vis_self_kept, region_live, vis_self_back, vis_grad)
    vis_self_grads = reduce_attention(vis_self_grads)
    cross_back = attention_params_again(0)
    lang_sum_grad, lang_context_grad, lang_out_w, lang_out_off, lang_scale, lang_shift = (
        output_back(lang_cross_sum, lang_context, cross_back[1], cross_back[2], lang_grad)
    )
    vis_sum_grad, vis_context_grad, vis_out_w, vis_out_off, vis_scale, vis_shift = output_back(
        vis_cross_sum, vis_context, cross_back[1], cross_back[2], vis_grad
    )
    lang_query_grad, vis_key_grad, vis_value_grad = attention_back(
        lang_parts[0], vis_parts[1], vis_parts[2], region_live, lang_total, lang_context_grad
    )
    vis_query_grad, lang_key_grad, lang_value_grad = attention_back(
        vis_parts[0], lang_parts[1], lang_parts[2], word_live, vis_total, vis_context_grad
    )
    lang_rows, lang_weight_grad, lang_query_off, lang_value_off = three_way_back(
        words, cross_back[0], lang_query_grad, lang_key_grad, lang_value_grad
    )
    vis_rows, vis_weight_grad, vis_query_off, vis_value_off = three_way_back(
        regions, cross_back[0], vis_query_grad, vis_key_grad, vis_value_grad
    )
    cross_grads = reduce_attention(
        (
            lang_weight_grad + vis_weight_grad,
            lang_out_w + vis_out_w,
            jnp.stack(
                [
                    lang_query_off + vis_query_off,
                    lang_value_off + vis_value_off,
                    lang_out_off + vis_out_off,
                ]
            ),
            lang_scale + vis_scale,
            lang_shift + vis_shift,
        )
    )
    words_grad = lang_sum_grad + lang_rows
    regions_grad = vis_sum_grad + vis_rows
    return (
        lang_three.astype(jnp.bfloat16),
        vis_three.astype(jnp.bfloat16),
        words_grad,
        regions_grad,
        jnp.stack([cross_grads[0], lang_self_grads[0], vis_self_grads[0]]),
        jnp.stack([cross_grads[1], lang_self_grads[1], vis_self_grads[1]]),
        jnp.stack([cross_grads[2], lang_self_grads[2], vis_self_grads[2]]),
        jnp.stack([lang_ffn_grads[0], vis_ffn_grads[0]]),
        jnp.stack([lang_ffn_grads[1], vis_ffn_grads[1]]),
        jnp.stack([lang_ffn_grads[2], vis_ffn_grads[2]]),
        jnp.stack([lang_ffn_grads[3], vis_ffn_grads[3]]),
        jnp.stack(
            [
                cross_grads[3],
                lang_self_grads[3],
                vis_self_grads[3],
                lang_ffn_grads[4],
                vis_ffn_grads[4],
            ]
        ),
        jnp.stack(
            [
                cross_grads[4],
                lang_self_grads[4],
                vis_self_grads[4],
                lang_ffn_grads[5],
                vis_ffn_grads[5],
            ]
        ),
    )


def solution(mesh):
    placed = (
        P(("dp", "fsdp"), None, None),
        P(("dp", "fsdp"), None, None),
        P(("dp", "fsdp")),
        P(("dp", "fsdp")),
        P(None, None, "fsdp", None),
        P(None, "fsdp", None),
        P(None, None, "fsdp"),
        P(None, "fsdp", None),
        P(None, "fsdp"),
        P(None, "fsdp", None),
        P(None, "fsdp"),
        P(None, "fsdp"),
        P(None, "fsdp"),
        P(("dp", "fsdp"), None, None),
        P(("dp", "fsdp"), None, None),
    )
    return jax.shard_map(
        local,
        mesh=mesh,
        in_specs=placed,
        out_specs=(
            P(("dp", "fsdp"), None, None),
            P(("dp", "fsdp"), None, None),
            P(("dp", "fsdp"), None, None),
            P(("dp", "fsdp"), None, None),
            P(None, None, "fsdp", None),
            P(None, "fsdp", None),
            P(None, None, "fsdp"),
            P(None, "fsdp", None),
            P(None, "fsdp"),
            P(None, "fsdp", None),
            P(None, "fsdp"),
            P(None, "fsdp"),
            P(None, "fsdp"),
        ),
        check_vma=False,
    )
```

profile of v0, /device:TPU:1, one launch (start us, length us, event | category | flops | bytes accessed | tf_op | source)
XLA Modules:
  0.0 1916.0 jit_solution(13008070732315000614)
XLA Ops:
  17.4 28.4 %all-gather.1 = bf16[1,3,768]{1,0,2:T(2,128)(2,1)S(1)} all-gather(bf16[1,3,96]{1,0,2:T(2,128)(2,1)S(1)} %copy.468), channel_id=3, replica_groups=mesh['dp'=4,'fsdp'=8] {'fsdp'}, dimensions={2}, use_global_device_ids=true | all-gather | bytes 5184 | tf_op jit(solution)/shard_map/all_gather | solution.py:197
  57.3 30.4 %all-reduce.27 = (bf16[768]{0:T(1024)(128)(2,1)S(1)}, bf16[768]{0:T(1024)(128)(2,1)S(1)}, bf16[768]{0:T(1024)(128)(2,1)S(1)}, bf16[768]{0:T(1024)(128)(2,1)S(1)}...) all-reduce(bf16[768]{0:T(1024)(128)(2,1)S(1)} %dynamic-update-slice, ...), channel_id=6, replica_groups=mesh['dp'=4,'fsdp'=8] {'fsdp'}, use_global_device_ids=true, to_apply=%add.1 | all-reduce | flops 7680 | bytes 30720
  87.9 25.7 %all-gather.6 = bf16[1,3,768]{1,0,2:T(2,128)(2,1)S(1)} all-gather(bf16[1,3,96]{1,0,2:T(2,128)(2,1)S(1)} %copy.469), channel_id=8, replica_groups=mesh['dp'=4,'fsdp'=8] {'fsdp'}, dimensions={2}, use_global_device_ids=true | all-gather | bytes 5184 | tf_op jit(solution)/shard_map/all_gather | solution.py:197
  145.7 26.1 %all-gather.17 = bf16[1,3,768]{1,0,2:T(2,128)(2,1)S(1)} all-gather(bf16[1,3,96]{1,0,2:T(2,128)(2,1)S(1)} %copy.470), channel_id=19, replica_groups=mesh['dp'=4,'fsdp'=8] {'fsdp'}, dimensions={2}, use_global_device_ids=true | all-gather | bytes 5184 | tf_op jit(solution)/shard_map/all_gather | solution.py:197
  230.8 29.7 %all-gather.50.cloned.1.call-done = bf16[1,3,768,768]{3,2,1,0:T(8,128)(2,1)} async-done(((bf16[1,3,96,768]{3,2,1,0:T(8,128)(2,1)}), bf16[1,3,768,768]{3,2,1,0:T(8,128)(2,1)}) %all-gather.50.cloned.1.call-update) | async-done | bytes 3538960 | tf_op jit(solution)/shard_map/all_gather | solution.py:195
  274.7 28.1 %all-gather.44.cloned.1.call-done = bf16[1,768,768]{2,1,0:T(8,128)(2,1)} async-done(((bf16[1,96,768]{2,1,0:T(8,128)(2,1)}), bf16[1,768,768]{2,1,0:T(8,128)(2,1)}) %all-gather.44.cloned.1.call-update) | async-done | bytes 1179664 | tf_op jit(solution)/shard_map/all_gather | solution.py:196
  348.9 77.1 %all-gather.46.cloned.1.call-done = bf16[1,768,3072]{2,1,0:T(8,128)(2,1)} async-done(((bf16[1,96,3072]{2,1,0:T(8,128)(2,1)}), bf16[1,768,3072]{2,1,0:T(8,128)(2,1)}) %all-gather.46.cloned.1.call-update) | async-done | bytes 4718608 | tf_op jit(solution)/shard_map/all_gather | solution.py:211
  434.2 71.7 %all-gather.48.cloned.1.call-done = bf16[1,3072,768]{2,1,0:T(8,128)(2,1)} async-done(((bf16[1,384,768]{2,1,0:T(8,128)(2,1)}), bf16[1,3072,768]{2,1,0:T(8,128)(2,1)}) %all-gather.48.cloned.1.call-update) | async-done | bytes 4718608 | tf_op jit(solution)/shard_map/all_gather | solution.py:213
  525.4 60.9 %all-gather.54.cloned.1.call-done = bf16[1,768,3072]{2,1,0:T(8,128)(2,1)} async-done(((bf16[1,96,3072]{2,1,0:T(8,128)(2,1)}), bf16[1,768,3072]{2,1,0:T(8,128)(2,1)}) %all-gather.54.cloned.1.call-update) | async-done | bytes 4718608 | tf_op jit(solution)/shard_map/all_gather | solution.py:211
  597.6 68.5 %all-gather.56.cloned.1.call-done = bf16[1,3072,768]{2,1,0:T(8,128)(2,1)} async-done(((bf16[1,384,768]{2,1,0:T(8,128)(2,1)}), bf16[1,3072,768]{2,1,0:T(8,128)(2,1)}) %all-gather.56.cloned.1.call-update) | async-done | bytes 4718608 | tf_op jit(solution)/shard_map/all_gather | solution.py:213
  849.3 31.1 %all-reduce.26 = (bf16[768]{0:T(1024)(128)(2,1)S(1)}, bf16[768]{0:T(1024)(128)(2,1)S(1)}, bf16[3072]{0:T(1024)(128)(2,1)S(1)}, bf16[3072]{0:T(1024)(128)(2,1)S(1...) all-reduce(bf16[768]{0:T(1024)(128)(2,1)S(1)} %copy-done.215, ...), channel_id=17, replica_groups=mesh['dp'=4,'fsdp'=8] {'fsdp'}, use_global_device_ids=true, to_apply=%add.6 | all-reduce | flops 16896 | bytes 67584
  885.0 45.3 %reduce-scatter.42.cloned.1.call-done = bf16[96,2304]{1,0:T(8,128)(2,1)} async-done(((bf16[768,2304]{1,0:T(8,128)(2,1)}), bf16[96,2304]{1,0:T(8,128)(2,1)}) %reduce-scatter.42.cloned.1.call-update) | async-done | bytes 442384
  933.2 79.9 %reduce-scatter.44.cloned.1.call-done = bf16[96,2304]{1,0:T(8,128)(2,1)} async-done(((bf16[768,2304]{1,0:T(8,128)(2,1)}), bf16[96,2304]{1,0:T(8,128)(2,1)}) %reduce-scatter.44.cloned.1.call-update) | async-done | bytes 442384
  1015.8 63.5 %reduce-scatter.26.cloned.1.call-done = bf16[96,768]{1,0:T(8,128)(2,1)} async-done(((bf16[768,768]{1,0:T(8,128)(2,1)}), bf16[96,768]{1,0:T(8,128)(2,1)}) %reduce-scatter.26.cloned.1.call-update) | async-done | bytes 147472 | tf_op jit(solution)/shard_map/reduce_scatter | solution.py:231
  1079.3 67.7 %reduce-scatter.30.cloned.1.call-done = bf16[96,768]{1,0:T(8,128)(2,1)} async-done(((bf16[768,768]{1,0:T(8,128)(2,1)}), bf16[96,768]{1,0:T(8,128)(2,1)}) %reduce-scatter.30.cloned.1.call-update) | async-done | bytes 147472 | tf_op jit(solution)/shard_map/reduce_scatter | solution.py:231
  1147.0 67.0 %reduce-scatter.28.cloned.1.call-done = bf16[96,768]{1,0:T(8,128)(2,1)} async-done(((bf16[768,768]{1,0:T(8,128)(2,1)}), bf16[96,768]{1,0:T(8,128)(2,1)}) %reduce-scatter.28.cloned.1.call-update) | async-done | bytes 147472 | tf_op jit(solution)/shard_map/reduce_scatter | solution.py:231
  1214.1 99.7 %reduce-scatter.36.cloned.1.call-done = bf16[384,768]{1,0:T(8,128)(2,1)} async-done(((bf16[3072,768]{1,0:T(8,128)(2,1)}), bf16[384,768]{1,0:T(8,128)(2,1)}) %reduce-scatter.36.cloned.1.call-update) | async-done | bytes 589840 | tf_op jit(solution)/shard_map/reduce_scatter | solution.py:260
  1313.8 98.8 %reduce-scatter.38.cloned.1.call-done = bf16[384,768]{1,0:T(8,128)(2,1)} async-done(((bf16[3072,768]{1,0:T(8,128)(2,1)}), bf16[384,768]{1,0:T(8,128)(2,1)}) %reduce-scatter.38.cloned.1.call-update) | async-done | bytes 589840 | tf_op jit(solution)/shard_map/reduce_scatter | solution.py:260
  1412.6 98.9 %reduce-scatter.34.cloned.1.call-done = bf16[96,3072]{1,0:T(8,128)(2,1)} async-done(((bf16[768,3072]{1,0:T(8,128)(2,1)}), bf16[96,3072]{1,0:T(8,128)(2,1)}) %reduce-scatter.34.cloned.1.call-update) | async-done | bytes 589840 | tf_op jit(solution)/shard_map/reduce_scatter | solution.py:254
  1511.6 98.8 %reduce-scatter.32.cloned.1.call-done = bf16[96,3072]{1,0:T(8,128)(2,1)} async-done(((bf16[768,3072]{1,0:T(8,128)(2,1)}), bf16[96,3072]{1,0:T(8,128)(2,1)}) %reduce-scatter.32.cloned.1.call-update) | async-done | bytes 589840 | tf_op jit(solution)/shard_map/reduce_scatter | solution.py:254
  1613.1 60.7 %reduce-scatter.46.cloned.1.call-done = bf16[96,3]{1,0:T(8,128)(2,1)} async-done(((bf16[768,3]{1,0:T(8,128)(2,1)}), bf16[96,3]{1,0:T(8,128)(2,1)}) %reduce-scatter.46.cloned.1.call-update) | async-done | bytes 592
  1674.5 63.5 %reduce-scatter.48.cloned.1.call-done = bf16[96,3]{1,0:T(8,128)(2,1)} async-done(((bf16[768,3]{1,0:T(8,128)(2,1)}), bf16[96,3]{1,0:T(8,128)(2,1)}) %reduce-scatter.48.cloned.1.call-update) | async-done | bytes 592
  1738.9 63.5 %reduce-scatter.50.cloned.1.call-done = bf16[96,3]{1,0:T(8,128)(2,1)} async-done(((bf16[768,3]{1,0:T(8,128)(2,1)}), bf16[96,3]{1,0:T(8,128)(2,1)}) %reduce-scatter.50.cloned.1.call-update) | async-done | bytes 592
  1817.9 80.9 %all-reduce.32.cloned.1.call-done = (bf16[1,3,96,768]{2,3,1,0:T(8,128)(2,1)}, bf16[1,3,96,768]{2,3,1,0:T(8,128)(2,1)}, bf16[1,3,96,768]{2,3,1,0:T(8,128)(2,1)}, ...) async-done(((bf16[1,3,96,768]{2,3,1,0:T(8,128)(2,1)}, ...) | async-done | bytes 4128784 | tf_op jit(solution)/shard_map/psum | solution.py:245
  (889 shorter events, 430.1 us)
Async XLA Ops:
  7.2 199.0 %all-gather.38.cloned.1.call-start = ((), (), s32[]{:S(2)}) async-start(), calls=%async_computation.20 | async-start | bytes 3981312 | tf_op jit(solution)/shard_map/all_gather | solution.py:195
  9.7 206.4 %all-gather.40.cloned.1.call-start = ((), (), s32[]{:S(2)}) async-start(), calls=%async_computation.21 | async-start | bytes 1327104 | tf_op jit(solution)/shard_map/all_gather | solution.py:196
  10.5 207.7 %all-gather.42.cloned.1.call-start = ((), (), s32[]{:S(2)}) async-start(), calls=%async_computation.22 | async-start | bytes 3981312 | tf_op jit(solution)/shard_map/all_gather | solution.py:195
  11.3 249.3 %all-gather.50.cloned.1.call-start = ((), (), s32[]{:S(2)}) async-start(), calls=%async_computation.26 | async-start | bytes 3981312 | tf_op jit(solution)/shard_map/all_gather | solution.py:195
  11.8 291.0 %all-gather.44.cloned.1.call-start = ((), (), s32[]{:S(2)}) async-start(), calls=%async_computation.23 | async-start | bytes 1327104 | tf_op jit(solution)/shard_map/all_gather | solution.py:196
  12.4 332.9 %all-gather.52.cloned.1.call-start = ((), (), s32[]{:S(2)}) async-start(), calls=%async_computation.27 | async-start | bytes 1327104 | tf_op jit(solution)/shard_map/all_gather | solution.py:196
  13.0 413.0 %all-gather.46.cloned.1.call-start = ((), (), s32[]{:S(2)}) async-start(), calls=%async_computation.24 | async-start | bytes 5308416 | tf_op jit(solution)/shard_map/all_gather | solution.py:211
  14.2 491.7 %all-gather.48.cloned.1.call-start = ((), (), s32[]{:S(2)}) async-start(), calls=%async_computation.25 | async-start | bytes 5308416 | tf_op jit(solution)/shard_map/all_gather | solution.py:213
  15.8 570.5 %all-gather.54.cloned.1.call-start = ((), (), s32[]{:S(2)}) async-start(), calls=%async_computation.28 | async-start | bytes 5308416 | tf_op jit(solution)/shard_map/all_gather | solution.py:211
  16.5 649.6 %all-gather.56.cloned.1.call-start = ((), (), s32[]{:S(2)}) async-start(), calls=%async_computation.29 | async-start | bytes 5308416 | tf_op jit(solution)/shard_map/all_gather | solution.py:213
  17.1 865.1 %reduce-scatter.40.cloned.1.call-start = ((), (), s32[]{:S(2)}) async-start(), calls=%async_computation.30 | async-start | bytes 3981312
  768.1 162.3 %reduce-scatter.42.cloned.1.call-start = ((), (), s32[]{:S(2)}) async-start(), calls=%async_computation.31 | async-start | bytes 3981312
  785.4 227.6 %reduce-scatter.44.cloned.1.call-start = ((), (), s32[]{:S(2)}) async-start(), calls=%async_computation.32 | async-start | bytes 3981312
  803.1 276.2 %reduce-scatter.26.cloned.1.call-start = ((), (), s32[]{:S(2)}) async-start(), calls=%async_computation.13 | async-start | bytes 1327104 | tf_op jit(solution)/shard_map/reduce_scatter | solution.py:231
  806.2 340.8 %reduce-scatter.30.cloned.1.call-start = ((), (), s32[]{:S(2)}) async-start(), calls=%async_computation.15 | async-start | bytes 1327104 | tf_op jit(solution)/shard_map/reduce_scatter | solution.py:231
  808.9 405.1 %reduce-scatter.28.cloned.1.call-start = ((), (), s32[]{:S(2)}) async-start(), calls=%async_computation.14 | async-start | bytes 1327104 | tf_op jit(solution)/shard_map/reduce_scatter | solution.py:231
  811.4 502.4 %reduce-scatter.36.cloned.1.call-start = ((), (), s32[]{:S(2)}) async-start(), calls=%async_computation.18 | async-start | bytes 5308416 | tf_op jit(solution)/shard_map/reduce_scatter | solution.py:260
  816.3 596.3 %reduce-scatter.38.cloned.1.call-start = ((), (), s32[]{:S(2)}) async-start(), calls=%async_computation.19 | async-start | bytes 5308416 | tf_op jit(solution)/shard_map/reduce_scatter | solution.py:260
  822.3 689.3 %reduce-scatter.34.cloned.1.call-start = ((), (), s32[]{:S(2)}) async-start(), calls=%async_computation.17 | async-start | bytes 5308416 | tf_op jit(solution)/shard_map/reduce_scatter | solution.py:254
  828.3 782.1 %reduce-scatter.32.cloned.1.call-start = ((), (), s32[]{:S(2)}) async-start(), calls=%async_computation.16 | async-start | bytes 5308416 | tf_op jit(solution)/shard_map/reduce_scatter | solution.py:254
  833.0 840.7 %reduce-scatter.46.cloned.1.call-start = ((), (), s32[]{:S(2)}) async-start(), calls=%async_computation.33 | async-start | bytes 221184
  841.6 896.5 %reduce-scatter.48.cloned.1.call-start = ((), (), s32[]{:S(2)}) async-start(), calls=%async_computation.34 | async-start | bytes 221184
  842.5 959.8 %reduce-scatter.50.cloned.1.call-start = ((), (), s32[]{:S(2)}) async-start(), calls=%async_computation.35 | async-start | bytes 221184
  843.5 1055.4 %all-reduce.32.cloned.1.call-start = ((), (), s32[]{:S(2)}) async-start(), calls=%async_computation.36 | async-start | bytes 9142272 | tf_op jit(solution)/shard_map/psum | solution.py:245
  (250 other events, 4477.4 us)
Sparse Core Ops, SparseCore 0:
  10.8 68.0 all-gather.37
  81.7 42.5 all-gather.39
  127.1 66.6 all-gather.41
  196.3 64.1 all-gather.49
  262.6 40.2 all-gather.43
  305.5 39.8 all-gather.51
  348.1 77.8 all-gather.45
  428.1 77.6 all-gather.47
  508.6 77.6 all-gather.53
  588.4 77.6 all-gather.55
  768.2 78.6 reduce-scatter.39
  850.4 79.9 reduce-scatter.41
  934.0 79.0 reduce-scatter.43
  1016.3 62.9 reduce-scatter.25
  1083.1 63.8 reduce-scatter.29
  1150.3 63.7 reduce-scatter.27
  1217.6 96.2 reduce-scatter.35
  1317.3 95.2 reduce-scatter.37
  1416.3 95.2 reduce-scatter.33
  1515.1 95.2 reduce-scatter.31
  1613.6 60.0 reduce-scatter.45
  1677.0 61.0 reduce-scatter.47
  1741.3 60.9 reduce-scatter.49
  1806.5 92.3 all-reduce.31
where the time goes:
time: 1930 us; the launch traced here: 1920 us
  waiting for transfers between devices  1350 us (70%)
  blocking collectives  199 us (10%)
  local copies, waits for them, and re-layouts  181 us (9%)
  matrix products  120 us (6%)
  other arithmetic  41.4 us (2%)
  between operations  19.8 us (1%)
    unnamed x30, waiting for transfers between devices  317 us
    reduce_scatter x2, waiting for transfers between devices, reduce_ffn(): lax.psum_scatter(grads[2].astype(jnp.bfloat16), 'fsdp', scatter_dimension...  199 us
    reduce_scatter x3, waiting for transfers between devices, reduce_attention(): lax.psum_scatter(grads[1].astype(jnp.bfloat16), 'fsdp', scatter_dimension...  198 us
    reduce_scatter x2, waiting for transfers between devices, reduce_ffn(): lax.psum_scatter(grads[0].astype(jnp.bfloat16), 'fsdp', scatter_dimension...  198 us
    all_gather x2, waiting for transfers between devices, ffn_params(): lax.all_gather(ffn_out[stream], 'fsdp', axis=0, tiled=True)  140 us
    all_gather x2, waiting for transfers between devices, ffn_params(): lax.all_gather(ffn_in[stream], 'fsdp', axis=0, tiled=True)  138 us
    dot_general x60, matrix products, product(): return jnp.einsum(pattern, left, right, preferred_element_type=jnp.float32)  120 us
    unnamed x564, local copies, waits for them, and re-layouts  99.2 us
  transfers between devices with their start and end apart: 24, of which 20 were waited for; matrix products, arithmetic and copies ran while one was open for 11% of the time, Pallas kernels for 0%

commit v1 on v0

v1 whole, which is shorter than its diff:
```python
import functools
import math
from types import SimpleNamespace

import jax
import jax.numpy as jnp
from jax import lax
from jax.experimental import pallas as pl
from jax.experimental.pallas import tpu as pltpu
from jax.sharding import PartitionSpec as P

HEADS = 12
HEAD_DIM = 64
EPS = 1e-06
NEG = -1e30
OUTER = 4
VECTORS = 24
AHEAD = 3
BF16 = jnp.bfloat16
F32 = jnp.float32
MESH = pl.DeviceIdType.MESH
S = (0, 1)
NN = ((1,), (0,))
NT = ((1,), (1,))
TN = ((0,), (0,))


def window(size, devices):
    worst = max((size * f) % 128 for f in range(devices))
    return -(-(size + worst) // 128) * 128


def al(value, step=128):
    return pl.multiple_of(value, step)


def rcopy(src, dst, send, recv, device):
    return pltpu.make_async_remote_copy(
        src_ref=src, dst_ref=dst, send_sem=send, recv_sem=recv, device_id=device, device_id_type=MESH
    )


def dot(a, b, dims):
    return lax.dot_general(a, b, (dims, ((), ())), preferred_element_type=F32)


def spaces(tree):
    if isinstance(tree, dict):
        return SimpleNamespace(**{k: spaces(v) for k, v in tree.items()})
    if isinstance(tree, list):
        return [spaces(v) for v in tree]
    return tree


def tiles(count, body):
    def run(t, carry):
        body(t)
        return carry

    lax.fori_loop(0, count, run, 0)


def add_rows(into, terms, rows, fresh=False):
    step = 32 if rows % 32 == 0 else 16 if rows % 16 == 0 else 8

    def body(i):
        at = pl.ds(al(i * step, step), step)
        value = None if fresh else into[at, :].astype(F32)
        for term in terms:
            more = term[at, :].astype(F32)
            value = more if value is None else value + more
        into[at, :] = value.astype(BF16)

    tiles(rows // step, body)


class Place:
    def __init__(self, fsdp):
        self.A, self.F = OUTER, fsdp
        self.B = fsdp // OUTER
        r, f = lax.axis_index("dp"), lax.axis_index("fsdp")
        self.r, self.f = r, f
        self.c, self.y = lax.rem(r, 2), lax.rem(r // 2, 2)
        self.o, self.b = f // self.B, lax.rem(f, self.B)
        self.core_peer = (r + 1 - 2 * self.c, f)
        self.y_peer = (r + 2 - 4 * self.y, f)
        self.far_peer = (r + 3 - 4 * self.y - 2 * self.c, f)

    def out_at(self, o):
        return (self.r, o * self.B + self.b)

    def out_peer(self, d):
        return self.out_at(lax.rem(self.o + d, self.A))

    def in_peer(self, d):
        return (self.r, self.o * self.B + lax.rem(self.b + d, self.B))

    def peers(self):
        return (
            [self.core_peer, self.y_peer, self.far_peer]
            + [self.out_peer(d) for d in range(1, self.A)]
            + [self.in_peer(d) for d in range(1, self.B)]
        )


class Ways:
    def __init__(self, outer, middle, step=128):
        self.outer, self.middle, self.step = outer, middle, step

    def own(self, y):
        at = y * (self.outer + self.middle)
        return (al(at, self.step) if self.step > 1 else at), self.outer

    def both(self):
        return self.outer, self.middle

    def other(self, y):
        return self.own(1 - y)


class Tensor:
    def __init__(self, g, t, src, view, rows, half, ways, sems, bufs, out, whole=None):
        self.g, self.t, self.src, self.view, self.whole = g, t, src, view, whole
        self.rs, self.split, self.ways, self.sems, self.bufs, self.out = rows, half, ways, sems, bufs, out
        self.private = whole is None
        self.qs = (1,) if self.private else (0, 1)
        self.stages = 3 if self.private else 6

    def sem(self, array, *at):
        return array.at[(self.t, *at)]

    def keys(self):
        g = self.g
        if self.split:
            return [(k, g.c * (g.A // 2) + k) for k in range(g.A // 2)]
        return [(d, lax.rem(g.o + g.A - d, g.A)) for d in (0, 2, 3, 1)[: g.A]]

    def row(self, o, b):
        g = self.g
        at = (o * g.B + b) * self.rs
        if self.split:
            at = lax.rem(at, (g.F // 2) * self.rs)
        return al(at, 8)

    def inset(self):
        return self.g.o // (self.g.A // 2) == self.g.c

    def mine(self, fn):
        if self.split:
            pl.when(self.inset())(fn)
        else:
            fn()

    def others(self, fn):
        if self.split:
            pl.when(jnp.logical_not(self.inset()))(fn)
        else:
            fn()

    def cols(self, q, back=False):
        way = self.ways
        return way.own(self.g.y) if q == 0 else way.both()

    def part(self, q, o, b, back=False):
        return self.view(self.row(o, b), self.rs, *self.cols(q, back))


    def own_copy(self, q):
        g = self.g
        return pltpu.make_async_copy(
            self.src(*self.cols(q)), self.part(q, g.o, g.b), self.sem(self.sems.own, q)
        )

    def zcopy(self, q, d):
        g = self.g
        slot = lax.rem(g.o, g.A // 2) if self.split else d - 1
        return rcopy(
            self.src(*self.cols(q)),
            self.part(q, g.o, g.b),
            self.sem(self.sems.zs, q, d - 1),
            self.sem(self.sems.zr, q, slot),
            g.out_peer(d),
        )

    def xcopy(self, q, d, k, o, from_src=False):
        g = self.g
        v = self.part(q, o, g.b)
        i = (d - 1) * g.A + k
        return rcopy(
            self.src(*self.cols(q)) if from_src else v,
            v,
            self.sem(self.sems.xs, q, i),
            self.sem(self.sems.xr, q, i),
            g.in_peer(d),
        )

    def ycopy(self, k, o):
        g = self.g
        v = self.view(self.row(o, 0), self.rs * g.B, *self.cols(0))
        return rcopy(v, v, self.sem(self.sems.ys, k), self.sem(self.sems.yr, k), g.y_peer)

    def own_slot(self):
        return lax.rem(self.g.o, self.g.A // 2) if self.split else 0

    def start_z(self):
        def go():
            for q in self.qs:
                for d in (2, 3, 1)[: self.g.A - 1]:
                    self.zcopy(q, d).start()

        self.mine(go)

    def start_x(self):
        g = self.g

        def go():
            for q in self.qs:
                self.own_copy(q).start()
                for d in range(1, g.B):
                    self.xcopy(q, d, self.own_slot(), g.o, True).start()

        self.mine(go)

    def forward_x(self):
        g = self.g
        for q in self.qs:
            for k, o in self.keys():

                def go(k=k, o=o, q=q):
                    v = self.part(q, o, g.b)
                    slot = k if self.split else k - 1
                    rcopy(
                        v, v, self.sem(self.sems.zs, q, 0), self.sem(self.sems.zr, q, slot), g.out_peer(1)
                    ).wait_recv()
                    for d in range(1, g.B):
                        self.xcopy(q, d, k, o).start()

                if self.split:
                    pl.when(o != g.o)(go)
                elif k > 0:
                    go()

    def x_arrived(self, q, k, o):
        g = self.g
        for d in range(1, g.B):
            v = self.part(q, o, lax.rem(g.b + g.B - d, g.B))
            i = (d - 1) * g.A + k
            rcopy(v, v, self.sem(self.sems.xs, q, i), self.sem(self.sems.xr, q, i), g.in_peer(1)).wait_recv()

    def forward_y0(self):
        g = self.g

        def go():
            k = self.own_slot()
            self.own_copy(0).wait()
            self.x_arrived(0, k, g.o)
            self.ycopy(k, g.o).start()

        self.mine(go)

    def forward_y(self):
        g = self.g
        for k, o in self.keys():

            def go(k=k, o=o):
                self.x_arrived(0, k, o)
                self.ycopy(k, o).start()

            if self.split:
                pl.when(o != g.o)(go)
            elif k > 0:
                go()

    def arrived(self):
        g = self.g
        self.mine(lambda: self.own_copy(1).wait())
        for k, o in self.keys():
            self.x_arrived(1, k, o)
            if not self.private:
                v = self.view(self.row(o, 0), self.rs * g.B, *self.ways.other(g.y))
                rcopy(v, v, self.sem(self.sems.ys, k), self.sem(self.sems.yr, k), g.y_peer).wait_recv()

    def drain(self):
        g = self.g

        def go():
            for q in self.qs:
                for d in range(1, g.A):
                    self.zcopy(q, d).wait_send()

        self.mine(go)
        for k, o in self.keys():
            for q in self.qs:
                for d in range(1, g.B):
                    self.xcopy(q, d, k, o).wait_send()
            if not self.private:
                self.ycopy(k, o).wait_send()


    def total_rows(self):
        return self.rs * (self.g.F // 2 if self.split else self.g.F)

    def owners(self):
        g = self.g
        if self.split:
            return [(k, g.c * (g.A // 2) + k) for k in range(g.A // 2)]
        return [(d, lax.rem(g.o + d, g.A)) for d in (2, 3, 1, 0)]

    def back_y(self):
        g = self.g
        v = self.view(0, self.total_rows(), *self.ways.other(g.y))
        return rcopy(v, self.bufs.y, self.sem(self.sems.gys), self.sem(self.sems.gyr), g.y_peer)

    def back_x(self, q, d, k, o, b):
        g = self.g
        i = (d - 1) * g.A + k
        return rcopy(
            self.part(q, o, b, True),
            self.bufs.x[q].at[i],
            self.sem(self.sems.gxs, q, i),
            self.sem(self.sems.gxr, q, i),
            g.in_peer(d),
        )

    def back_z(self, q, k, o):
        g = self.g
        slot = lax.rem(o - g.o + g.A, g.A) - 1 if self.split else k - 1
        return rcopy(
            self.part(q, o, g.b, True),
            self.bufs.z[q].at[slot],
            self.sem(self.sems.gzs, q, k if self.split else k - 1),
            self.sem(self.sems.gzr, q, slot),
            g.out_at(o),
        )

    def each_z(self, q, k, o, way):
        if self.split:
            pl.when(o != self.g.o)(lambda: way(self.back_z(q, k, o)))
        elif k > 0:
            way(self.back_z(q, k, o))

    def back_y2(self, q):
        g = self.g
        return rcopy(
            self.part(q, g.o, g.b, True),
            self.bufs.y2[q],
            self.sem(self.sems.gws, q),
            self.sem(self.sems.gwr, q),
            g.y_peer,
        )

    def back_core(self):
        g = self.g
        return rcopy(
            self.whole(self.row(g.o, g.b), self.rs),
            self.bufs.c,
            self.sem(self.sems.gcs),
            self.sem(self.sems.gcr),
            g.core_peer,
        )

    def put_own(self):
        g = self.g
        return pltpu.make_async_copy(
            self.whole(self.row(g.o, g.b), self.rs), self.out(g.c), self.sem(self.sems.put, 0)
        )

    def put_other(self):
        return pltpu.make_async_copy(self.bufs.c, self.out(1 - self.g.c), self.sem(self.sems.put, 1))

    def fin(self, i):
        g = self.g
        return rcopy(
            self.part(1, g.o, g.b),
            self.bufs.fin.at[i],
            self.sem(self.sems.fs, i),
            self.sem(self.sems.fr, i),
            (g.core_peer, g.y_peer, g.far_peer)[i],
        )

    def put(self, i):
        g = self.g
        c = (1 - g.c, g.c, 1 - g.c, g.c)[i]
        y = (g.y, 1 - g.y, 1 - g.y, g.y)[i]
        source = self.part(1, g.o, g.b) if i == 3 else self.bufs.fin.at[i]
        return pltpu.make_async_copy(source, self.out(y, c), self.sem(self.sems.put, i))

    def taken(self):
        return ((1,), (0, 2)) if self.split else ((0, 1, 2), ())

    def send(self):
        if not self.private:
            self.back_y().start()
        self.send_x(1)

    def send_x(self, q, only=None):
        g = self.g
        for k, o in self.owners():
            if only is None or k == only:
                for d in range(1, g.B):
                    self.back_x(q, d, k, o, lax.rem(g.b + d, g.B)).start()

    def take_y(self):
        self.back_y().wait_recv()
        rows = self.total_rows()
        add_rows(self.view(0, rows, *self.cols(0, True)), [self.bufs.y], rows)
        self.send_x(0)

    def take_x(self, q):
        g = self.g
        for k, o in self.owners():
            terms = []
            for d in range(1, g.B):
                self.back_x(q, d, k, o, g.b).wait_recv()
                terms.append(self.bufs.x[q].at[(d - 1) * g.A + k])
            if terms:
                add_rows(self.part(q, o, g.b, True), terms, self.rs)
            self.each_z(q, k, o, lambda copy: copy.start())

    def take_z(self, q):
        g = self.g

        def go():
            v = self.part(q, g.o, g.b, True)
            for d in range(g.A - 1):
                rcopy(
                    v,
                    self.bufs.z[q].at[d],
                    self.sem(self.sems.gzs, q, 0),
                    self.sem(self.sems.gzr, q, d),
                    g.out_peer(1),
                ).wait_recv()
            add_rows(v, [self.bufs.z[q].at[d] for d in range(g.A - 1)], self.rs)
            if self.private:
                for i in range(3):
                    self.fin(i).start()
                self.put(3).start()
            else:
                self.back_y2(q).start()

        self.mine(go)

    def take_y2(self, q):
        g = self.g

        def go():
            self.back_y2(q).wait()
            if q == 1:
                add_rows(self.part(1, g.o, g.b, True), [self.bufs.y2[1]], self.rs)
            else:
                self.back_y().wait_send()
                at = self.view(self.row(g.o, g.b), self.rs, *self.ways.other(g.y))
                add_rows(at, [self.bufs.y2[0]], self.rs, fresh=True)
                self.back_core().start()
                self.put_own().start()

        self.mine(go)
        if q == 0 and self.split:
            self.others(lambda: self.back_y().wait_send())

    def take_core(self):
        def go():
            self.back_core().wait_recv()
            self.put_other().start()

        self.others(go)

    def take_fin(self):
        def go(which):
            for i in which:
                self.fin(i).wait_recv()
                self.put(i).start()

        self.mine(lambda: go(self.taken()[0]))
        self.others(lambda: go(self.taken()[1]))

    def stage(self, n):
        if self.private:
            if n == 0:
                self.take_x(1)
            elif n == 1:
                self.take_z(1)
            elif n == 2:
                self.take_fin()
        elif n == 0:
            self.take_y()
        elif n == 1:
            self.take_x(1)
        elif n == 2:
            self.take_x(0)
            self.take_z(1)
        elif n == 3:
            self.take_z(0)
            self.take_y2(1)
        elif n == 4:
            self.take_y2(0)
        elif n == 5:
            self.take_core()

    def finish(self):
        g = self.g
        for q in self.qs:
            for d in range(1, g.B):
                for k, o in self.owners():
                    self.back_x(q, d, k, o, g.b).wait_send()
            for k, o in self.owners():
                self.each_z(q, k, o, lambda copy: copy.wait_send())

        def mine():
            if self.private:
                for i in range(3):
                    self.fin(i).wait_send()
                for i in self.taken()[0] + (3,):
                    self.put(i).wait()
            else:
                self.back_core().wait_send()
                self.put_own().wait()

        def others():
            if self.private:
                for i in self.taken()[1]:
                    self.put(i).wait()
            else:
                self.put_other().wait()

        self.mine(mine)
        self.others(others)


def kernel(tree, sizes, *refs):
    inp, out, R = (spaces(part) for part in jax.tree.unflatten(tree, refs))
    F, D, FF, n, items = sizes
    g = Place(F)
    h, hf = D // 2, FF // 2
    scale = HEAD_DIM ** (-0.5)
    pairs = HEADS // 4
    sems = R.sem

    meet = pltpu.get_barrier_semaphore()
    peers = g.peers()
    for peer in peers:
        pl.semaphore_signal(meet, inc=1, device_id=peer, device_id_type=MESH)
    pl.semaphore_wait(meet, len(peers))

    rs, rf = D // F, FF // F
    line = []

    def make(*args):
        line.append(Tensor(g, len(line), *args))
        return line[-1]

    q0 = make(
        lambda j, k: inp.attn_qkv.at[0, j, :, pl.ds(al(g.c * h), h)],
        lambda r, k, j, kj: R.wq0.at[j, pl.ds(r, k), :],
        rs,
        False,
        Ways(1, 1, 1),
        sems,
        R.gq0,
        lambda c: out.q.at[0, :, :, pl.ds(al(c * h), h)],
        lambda r, k: R.wq0.at[:, pl.ds(r, k), :],
    )
    o0 = make(
        lambda j, k: inp.attn_out.at[0, :, pl.ds(j, k)],
        lambda r, k, j, kj: R.wo0.at[pl.ds(r, k), pl.ds(j, kj)],
        rs,
        True,
        Ways(D // 3, D // 3),
        sems,
        R.go0,
        lambda c: out.o.at[0],
        lambda r, k: R.wo0.at[pl.ds(r, k), :],
    )
    qp = [
        make(
            lambda j, k, i=i: inp.attn_qkv.at[1 + g.y, i, :, pl.ds(al(g.c * h), h)],
            lambda r, k, j, kj, i=i: R.wq.at[i, pl.ds(r, k), :],
            rs,
            False,
            Ways(0, h),
            sems,
            R.gq[i],
            lambda y, c, i=i: out.q.at[1 + y, i, :, pl.ds(al(c * h), h)],
        )
        for i in range(3)
    ]
    op = make(
        lambda j, k: inp.attn_out.at[1 + g.y],
        lambda r, k, j, kj: R.wo.at[pl.ds(r, k), :],
        rs,
        True,
        Ways(0, D),
        sems,
        R.go,
        lambda y, c: out.o.at[1 + y],
    )
    wide, long = hf // 2, D // 2
    ip = [
        make(
            lambda j, k, i=i: inp.ffn_in.at[g.y, :, pl.ds(al(g.c * hf + i * wide), wide)],
            lambda r, k, j, kj, i=i: R.wi.at[pl.ds(r, k), pl.ds(i * wide, wide)],
            rs,
            False,
            Ways(0, wide),
            sems,
            R.gi[i],
            lambda y, c, i=i: out.i.at[y, :, pl.ds(al(c * hf + i * wide), wide)],
        )
        for i in range(2)
    ]
    fp = [
        make(
            lambda j, k, i=i: inp.ffn_out.at[g.y, :, pl.ds(i * long, long)],
            lambda r, k, j, kj, i=i: R.wf.at[pl.ds(r, k), pl.ds(i * long, long)],
            rf,
            True,
            Ways(0, long),
            sems,
            R.gf[i],
            lambda y, c, i=i: out.f.at[y, :, pl.ds(i * long, long)],
        )
        for i in range(2)
    ]

    slot_of = lambda f: R.vec_in.at[f]

    def vec_z(d):
        return rcopy(inp.vectors, slot_of(g.f), sems.vzs.at[d - 1], sems.vzr.at[d - 1], g.out_peer(d))

    def vec_x(d, k):
        o = lax.rem(g.o + g.A - k, g.A)
        at = slot_of(o * g.B + g.b)
        i = (d - 1) * g.A + k
        return rcopy(inp.vectors if k == 0 else at, at, sems.vxs.at[i], sems.vxr.at[i], g.in_peer(d))

    for d in range(1, g.A):
        vec_z(d).start()
    for d in range(1, g.B):
        vec_x(d, 0).start()

    count = [0, 0]

    def exchange(src, dst, device=None, start=True):
        i = count[0]
        count[0] += 1
        copy = rcopy(src, dst, sems.es.at[i], sems.er.at[i], g.core_peer if device is None else device)
        if start:
            copy.start()
        return copy

    def load(src, dst, start=True):
        i = count[1]
        count[1] += 1
        copy = pltpu.make_async_copy(src, dst, sems.load.at[i])
        if start:
            copy.start()
        return copy

    def this(s):
        return g.y == s

    def that(s):
        return g.y != s

    x0_own = [load(inp.x[s], R.x0[s].at[pl.ds(0, n[s])]) for s in S]
    x0_other = [exchange(inp.x[s], R.x0[s].at[pl.ds(n[s], n[s])]) for s in S]

    def item_of(at, slots):
        return sum((at >= slots * i).astype(jnp.int32) for i in range(1, items))

    lane = lax.broadcasted_iota(jnp.int32, (8, 128 + n[1]), 1)
    slots = [n[s] // items for s in S]
    alive = jnp.zeros((8, 128 + n[1]), jnp.int32)
    for s in S:
        for i in range(items):
            start = 128 * s + slots[s] * i
            alive = alive + ((lane >= start) & (lane < start + inp.live[s][i])).astype(jnp.int32)
    R.keys[0] = jnp.where(alive > 0, 0.0, NEG)
    key_other = [
        exchange(R.keys.at[0], R.keys.at[i], device)
        for i, device in ((2, g.core_peer), (1, g.y_peer), (3, g.far_peer))
    ]
    vec_own = load(inp.vectors, slot_of(g.f))
    q0.start_z()
    q0.start_x()
    o0.start_z()
    o0.start_x()
    line[2].start_z()
    line[2].start_x()
    for x in line[3:]:
        x.start_z()
    cot_own = [load(inp.cot[s], R.cot.at[pl.ds(0, n[s])], False) for s in S]
    cot_other = [exchange(inp.cot[s], R.cot.at[pl.ds(n[s], n[s])], g.y_peer, False) for s in S]
    for s in S:
        pl.when(this(s))(cot_own[s].start)
        pl.when(that(s))(cot_other[s].start)

    for k in range(1, g.A):
        o = lax.rem(g.o + g.A - k, g.A)
        at = slot_of(o * g.B + g.b)
        rcopy(at, at, sems.vzs.at[0], sems.vzr.at[k - 1], g.out_peer(1)).wait_recv()
        for d in range(1, g.B):
            vec_x(d, k).start()
    for d in range(1, g.B):
        for k in range(g.A):
            o = lax.rem(g.o + g.A - k, g.A)
            at = slot_of(o * g.B + lax.rem(g.b + g.B - d, g.B))
            i = (d - 1) * g.A + k
            rcopy(at, at, sems.vxs.at[i], sems.vxr.at[i], g.in_peer(1)).wait_recv()
    vec_own.wait()
    vec, vin, grad = R.vec, R.vin, R.grad
    vec[...] = jnp.zeros_like(vec)
    vin[...] = jnp.zeros_like(vin)
    grad[...] = jnp.zeros_like(grad)
    for f in range(F):
        for into, low, high, size in ((vec, 0, VECTORS, D // F), (vin, VECTORS, VECTORS + 8, FF // F)):
            start, turn, span = size * f // 128 * 128, size * f % 128, window(size, F)
            piece = R.vec_in[f, low:high, 0:span].astype(F32)
            into[:, start : start + span] += pltpu.roll(piece, turn, 1) if turn else piece

    def row_of(i):
        return vec[i : i + 1, 0:D]

    ATT_BIAS, OUT_BIAS, GAIN, SHIFT = 0, 9, 11, 16

    for copy in key_other:
        copy.wait_recv()

    def build(b):
        lane = lax.broadcasted_iota(jnp.int32, (1, 128 + n[1]), 1)
        key_item = jnp.where(lane < 128, item_of(lane, n[0] // items), item_of(lane - 128, n[1] // items))
        for s in S:
            query_item = item_of(lax.broadcasted_iota(jnp.int32, (n[s], 1), 0), n[s] // items)
            rows = pl.ds(s * n[0], n[s])
            R.masks[b, rows, :] = jnp.where(query_item == key_item, R.keys[b, 0:1, :], NEG)

    tiles(4, build)
    for s in S:
        x0_own[s].wait()
    for s in S:
        x0_other[s].wait_recv()

    def project(m, x, wq, qkv):
        for j in range(3):
            value = dot(x[...], wq[j], NN)
            if j != 1:
                row = ATT_BIAS + 3 * m + (0 if j == 0 else 1)
                value = value + vec[row : row + 1, pl.ds(al(g.c * h), h)]
            qkv[j] = value.astype(BF16)

    def mask_of(b, qs, ks):
        return R.masks[b, pl.ds(qs * n[0], n[qs]), pl.ds(ks * 128, n[ks])]

    def attend(qs, ks, q_ref, kv_ref, probs, context, total):
        def body(b):
            qr, kr = pl.ds(al(b * n[qs], 16), n[qs]), pl.ds(al(b * n[ks], 16), n[ks])
            mask = mask_of(b * (4 // total), qs, ks)
            cut = lambda ref, j, rows, i: ref[j, rows, i * HEAD_DIM : (i + 1) * HEAD_DIM]
            heads = range(2 * pairs)
            scores = [dot(cut(q_ref, 0, qr, i), cut(kv_ref, 1, kr, i), NT) * scale + mask for i in heads]
            tops = [jnp.max(v, -1, keepdims=True) for v in scores]
            exs = [jnp.exp(v - top) for v, top in zip(scores, tops)]
            sums = [1.0 / jnp.sum(v, -1, keepdims=True) for v in exs]
            shares = [v * k for v, k in zip(exs, sums)]
            parts = [dot(pr.astype(BF16), cut(kv_ref, 2, kr, i), NN) for i, pr in enumerate(shares)]
            made = [jnp.concatenate(parts[2 * p : 2 * p + 2], 1).astype(BF16) for p in range(pairs)]
            for i, pr in enumerate(shares):
                probs[2 * pairs * b + i, 0 : n[qs], 0 : n[ks]] = pr
            for p, value in enumerate(made):
                context[qr, p * 128 : (p + 1) * 128] = value

        tiles(total, body)

    def attend_back(qs, ks, q_ref, kv_ref, probs, dc_ref, dq_ref, dkv_ref, m, total):
        def body(b):
            qr, kr = pl.ds(al(b * n[qs], 16), n[qs]), pl.ds(al(b * n[ks], 16), n[ks])
            cut = lambda ref, j, rows, i: ref[j, rows, i * HEAD_DIM : (i + 1) * HEAD_DIM]
            heads = range(2 * pairs)
            dcs = [dc_ref[qr, i * HEAD_DIM : (i + 1) * HEAD_DIM] for i in heads]
            prs = [probs[2 * pairs * b + i, 0 : n[qs], 0 : n[ks]] for i in heads]
            dps = [dot(d, cut(kv_ref, 2, kr, i), NT) for i, d in enumerate(dcs)]
            dvs = [dot(pr.astype(BF16), d, TN) for pr, d in zip(prs, dcs)]
            sums = [jnp.sum(pr * dp, -1, keepdims=True) for pr, dp in zip(prs, dps)]
            dss = [(pr * (dp - k)).astype(BF16) for pr, dp, k in zip(prs, dps, sums)]
            dqs = [dot(ds, cut(kv_ref, 1, kr, i), NN) * scale for i, ds in enumerate(dss)]
            dks = [dot(ds, cut(q_ref, 0, qr, i), TN) * scale for i, ds in enumerate(dss)]
            made = [[jnp.concatenate(v[2 * p : 2 * p + 2], 1) for v in (dqs, dks, dvs)] for p in range(pairs)]
            row = ATT_BIAS + 3 * m
            for p, (dq, dk, dv) in enumerate(made):
                cols = slice(p * 128, (p + 1) * 128)
                dq_ref[0, qr, cols] = dq.astype(BF16)
                dkv_ref[1, kr, cols] = dk.astype(BF16)
                dkv_ref[2, kr, cols] = dv.astype(BF16)
            for p, (dq, dk, dv) in enumerate(made):
                lanes = pl.ds(al(g.c * h + p * 128), 128)
                grad[row : row + 1, lanes] += jnp.sum(dq, 0, keepdims=True)
                grad[row + 1 : row + 2, lanes] += jnp.sum(dv, 0, keepdims=True)

        tiles(total, body)

    def halves(acc, sb, rb, product, step=256):
        rows = acc.shape[0]

        def body(t):
            cols = pl.ds(al(t * step), step)
            value = product(cols)
            acc[:, cols] = value[:rows]
            sb[:, cols] = value[rows:].astype(BF16)

        tiles(D // step, body)
        return exchange(sb, rb)

    def block(rows):
        return next(k for k in (48, 80, 32, 16) if rows % k == 0)

    def norm(base, acc, rb, xh, rr, k, bias, into):
        step = block(acc.shape[0])

        def body(i):
            at = pl.ds(al(i * step, 16), step)
            total = base(at) + ((acc[at, :] + rb[at, :].astype(F32)) + row_of(bias))
            centered = total - jnp.mean(total, -1, keepdims=True)
            spread = lax.rsqrt(jnp.mean(centered * centered, -1, keepdims=True) + EPS)
            xhat = centered * spread
            xh[at, :] = xhat
            rr[at, :] = jnp.broadcast_to(spread, (step, 128))
            into[at, :] = (xhat * row_of(GAIN + k) + row_of(SHIFT + k)).astype(BF16)

        tiles(acc.shape[0] // step, body)

    def norm_back(dy_of, ds, xh, rr, k, bias, f):
        rows = ds.shape[0]
        step = block(rows)

        def body(i, carry):
            at = pl.ds(al(i * step, 16), step)
            dy = dy_of(at)
            xhat = xh[at, :]
            dx = dy * row_of(GAIN + k)
            dyx = dy * xhat
            mean_dx = jnp.mean(dx, -1, keepdims=True)
            mean_dxx = jnp.mean(dx * xhat, -1, keepdims=True)
            dh = rr[at, 0:1] * (dx - mean_dx - xhat * mean_dxx)
            ds[at, :] = dh
            f[at, :] = dh.astype(BF16)
            fold = lambda v: sum(v[j : j + 8] for j in range(0, step, 8))
            return (carry[0] + fold(dyx), carry[1] + fold(dy), carry[2] + fold(dh))

        zero = jnp.zeros((8, D), F32)
        sums = lax.fori_loop(0, rows // step, body, (zero, zero, zero))
        for row, value in zip((GAIN + k, SHIFT + k, bias), sums):
            grad[row : row + 1, :] += jnp.sum(value, 0, keepdims=True)
        return exchange(f.at[pl.ds(0, rows)], f.at[pl.ds(rows, rows)])

    def hidden(s, i, x, gl, gp):
        def body(t):
            cols = pl.ds(al(i * wide + t * 256), 256)
            u = dot(x[...], R.wi[:, cols], NN) + vin[s : s + 1, pl.ds(al(g.c * hf + i * wide + t * 256), 256)]
            phi = 0.5 + 0.5 * lax.erf(u * (1.0 / math.sqrt(2.0)))
            gl[:, cols] = (u * phi).astype(BF16)
            gp[:, cols] = (phi + u * (jnp.exp(-0.5 * (u * u)) * (1.0 / math.sqrt(2.0 * math.pi)))).astype(BF16)

        tiles(wide // 256, body)

    def hidden_back(s, f, gl, gp, du, half):
        def body(i):
            t = half * (hf // 512) + i
            cols = pl.ds(al(t * 256), 256)
            value = dot(f[...], R.wf[cols, :], NT) * gp[:, cols].astype(F32)
            du[:, cols] = value.astype(BF16)
            per = D // 256
            row = VECTORS + s * (FF // D) + g.c * (hf // D) + t // per
            grad[pl.ds(row, 1), pl.ds(al(lax.rem(t, per) * 256), 256)] = jnp.sum(value, 0, keepdims=True)
            R.wf[cols, :] = dot(gl[:, cols], f[...], TN).astype(BF16)

        tiles(hf // 512, body)

    def hidden_weight(i, x, du):
        def body(t):
            cols = pl.ds(al(t * 128), 128)
            at = pl.ds(i * wide, wide)
            R.wi[cols, at] = dot(x[:, cols], du[:, at], TN).astype(BF16)

        tiles(D // 128, body)

    def context_back(f, wo, dc):
        def body(t):
            cols = pl.ds(al(t * 128), 128)
            dc[:, cols] = dot(f[...], wo[cols, :], NT).astype(BF16)

        tiles(h // 128, body)

    def out_weight(wo, fs, contexts):
        def body(t):
            cols = pl.ds(al(t * 128), 128)
            wo[cols, :] = sum(dot(c[:, cols], f[...], TN) for f, c in zip(fs, contexts)).astype(BF16)

        tiles(h // 128, body)

    def qkv_weight(wq, j, xs, dqs):
        def body(t):
            cols = pl.ds(al(t * 256), 256)
            wq[j, cols, :] = sum(dot(x[:, cols], dq[j], TN) for x, dq in zip(xs, dqs)).astype(BF16)

        tiles(D // 256, body)

    def qkv_back(acc, sb, rb, dq, wq):
        return halves(acc, sb, rb, lambda cols: sum(dot(dq[j], wq[j, cols, :], NT) for j in range(3)))

    def pump(i):
        line[i].forward_x()
        if i + AHEAD < len(line):
            line[i + AHEAD].start_x()
        if i == 0:
            q0.forward_y0()
        elif i == 1:
            q0.forward_y()
            o0.forward_y0()
        elif i == 2:
            o0.forward_y()

    done = {}

    def step(*tensors):
        for x in tensors:
            x.stage(done.get(x.t, 0))
            done[x.t] = done.get(x.t, 0) + 1

    for i in range(3):
        pump(i)
    q0.arrived()
    for s in S:
        project(0, R.x0[s], R.wq0, R.qkv0[s])
    pump(3)
    attend(0, 1, R.qkv0[0], R.qkv0[1], R.p0[0], R.c0[0], 2)
    pump(4)
    attend(1, 0, R.qkv0[1], R.qkv0[0], R.p0[1], R.c0[1], 2)
    o0.arrived()
    part = [
        halves(R.acc[s], R.sb[s], R.rb[s], lambda cols, s=s: dot(R.c0[s][...], R.wo0[:, cols], NN)) for s in S
    ]
    pump(5)
    x1_own, x1_core, x1_y, x1_far = [], [], [], []
    for s in S:
        k = n[s]
        part[s].wait()
        norm(
            lambda at, s=s: R.x0[s][at, :].astype(F32),
            R.acc[s], R.rb[s], R.xh0[s], R.rr0[s], 0, ATT_BIAS + 2, R.x1o[s],
        )
        x1_own.append(load(R.x1o[s], R.x1.at[pl.ds(0, k)], False))
        x1_core.append(exchange(R.x1o[s], R.x1.at[pl.ds(2 * k, k)], None, False))
        x1_y.append(exchange(R.x1o[s], R.x1.at[pl.ds(k, k)], g.y_peer, False))
        x1_far.append(exchange(R.x1.at[pl.ds(k, k)], R.x1.at[pl.ds(3 * k, k)], None, False))

        def keep(s=s):
            x1_own[s].start()
            x1_core[s].start()

        pl.when(this(s))(keep)
        pl.when(that(s))(x1_y[s].start)

    def private(s):
        m, k = 1 + s, n[s]
        k2, k4 = 2 * k, 4 * k
        top = lambda ref, rows: ref.at[pl.ds(0, rows)]
        third = lambda ref: ref.at[:, pl.ds(0, k4)]
        x1, x2 = top(R.x1, k4), top(R.x2, k4)
        qkv, dq, ctx, dc = third(R.qkv), third(R.dq), top(R.c, k4), top(R.dc, k4)
        acc, sb, rb, ds = (top(v, k2) for v in (R.accp, R.sbp, R.rbp, R.dsp))
        gl, gp, du = (top(v, k4) for v in (R.g, R.gp, R.du))
        xh, rr = [R.xh.at[i, pl.ds(0, k2)] for i in S], [R.rr.at[i, pl.ds(0, k2)] for i in S]
        f1, f2 = (R.f.at[i, pl.ds(0, k4)] for i in S)
        x1_y[s].wait_recv()
        x1_far[s].start()
        x1_own[s].wait()
        x1_core[s].wait_recv()
        x1_far[s].wait_recv()
        for x in qp:
            x.arrived()
        project(m, x1, R.wq, qkv)
        pump(6)
        attend(s, s, qkv, qkv, R.p, ctx, 4)
        op.arrived()
        out1 = halves(acc, sb, rb, lambda cols: dot(ctx[...], R.wo[:, cols], NN))
        pump(7)
        out1.wait()
        norm(lambda at: x1[at, :].astype(F32), acc, rb, xh[0], rr[0], 1 + s, ATT_BIAS + 3 * m + 2, top(x2, k2))
        x2_core = exchange(top(x2, k2), x2.at[pl.ds(k2, k2)])
        ip[0].arrived()
        x2_core.wait_recv()
        hidden(s, 0, x2, gl, gp)
        pump(8)
        ip[1].arrived()
        hidden(s, 1, x2, gl, gp)
        pump(9)
        for x in fp:
            x.arrived()
        out2 = halves(acc, sb, rb, lambda cols: dot(gl[...], R.wf[:, cols], NN))
        out2.wait()
        norm(
            lambda at: xh[0][at, :] * row_of(GAIN + 1 + s) + row_of(SHIFT + 1 + s),
            acc, rb, xh[1], rr[1], 3 + s, OUT_BIAS + s, top(R.yp, k2),
        )
        y_out[s].start()
        cot_own[s].wait()
        cot_other[s].wait_recv()
        row_at = lax.broadcasted_iota(jnp.int32, (k, 128 + n[1]), 0) + 128 * s
        same = row_at == lax.broadcasted_iota(jnp.int32, (k, 128 + n[1]), 1)
        for i in S:
            value = jnp.sum(jnp.where(same, R.keys[i, 0:1, :], 0.0), -1, keepdims=True)
            R.row_live[i * k : (i + 1) * k, :] = jnp.broadcast_to(value, (k, 128))

        def cot_of(at):
            return jnp.where(R.row_live[at, 0:1] == 0.0, R.cot[at, :].astype(F32), 0.0)

        f_core = norm_back(cot_of, ds, xh[1], rr[1], 3 + s, OUT_BIAS + s, f2)
        for x in line:
            x.drain()
        f_core.wait()
        for half in range(2):
            hidden_back(s, f2, gl, gp, du, half)
            fp[0].send_x(1, half)
        fp[1].send()
        din = halves(acc, sb, rb, lambda cols: dot(du[...], R.wi[cols, :], NT))
        for i, x in enumerate(ip):
            hidden_weight(i, x2, du)
            x.send()
        din.wait()
        back = lambda at: ds[at, :] + (acc[at, :] + rb[at, :].astype(F32))
        f_core = norm_back(back, ds, xh[0], rr[0], 1 + s, ATT_BIAS + 3 * m + 2, f1)
        step(fp[0])
        f_core.wait()
        context_back(f1, R.wo, dc)
        out_weight(R.wo, [f1], [ctx])
        op.send()
        attend_back(s, s, qkv, qkv, R.p, dc, dq, dq, m, 4)
        step(fp[1])
        dx = qkv_back(acc, sb, rb, dq, R.wq)
        for j in range(3):
            qkv_weight(R.wq, j, [x1], [dq])
            qp[j].send()
        step(fp[0], ip[0])
        dx.wait()

        def split(i):
            at = pl.ds(al(i * 16, 16), 16)
            low = pl.ds(al(k + i * 16, 16), 16)
            R.dy[s][at, :] = back(at)
            R.dgive[at, :] = back(low).astype(BF16)

        tiles(k // 16, split)
        dy_give[s].start()
        step(fp[0], fp[1])
        x1_core[s].wait_send()
        x1_far[s].wait_send()
        x2_core.wait_send()
        x1_y[1 - s].wait_send()
        cot_other[1 - s].wait_send()

    y_out = [exchange(R.yp.at[pl.ds(n[s], n[s])], R.yin.at[pl.ds(0, n[s])], g.y_peer, False) for s in S]
    dy_give = [exchange(R.dgive.at[pl.ds(0, n[s])], R.dtake.at[pl.ds(0, n[s])], g.y_peer, False) for s in S]
    pl.when(this(0))(functools.partial(private, 0))
    done.clear()
    pl.when(this(1))(functools.partial(private, 1))

    f0 = []
    for s in S:

        def take(s=s):
            dy_give[s].wait_recv()

            def body(i):
                at = pl.ds(al(i * 16, 16), 16)
                R.dy[s][at, :] = R.dtake[at, :].astype(F32)

            tiles(n[s] // 16, body)

        pl.when(that(s))(take)
        f0.append(
            norm_back(lambda at, s=s: R.dy[s][at, :], R.ds[s], R.xh0[s], R.rr0[s], 0, ATT_BIAS + 2, R.f0[s])
        )
    step(ip[1])
    for s in S:
        f0[s].wait()
        context_back(R.f0[s], R.wo0, R.dc0[s])
    out_weight(R.wo0, R.f0, R.c0)
    o0.send()
    step(ip[0], op)
    attend_back(0, 1, R.qkv0[0], R.qkv0[1], R.p0[0], R.dc0[0], R.dq0[0], R.dq0[1], 0, 2)
    step(fp[1], ip[1], o0)
    attend_back(1, 0, R.qkv0[1], R.qkv0[0], R.p0[1], R.dc0[1], R.dq0[1], R.dq0[0], 0, 2)

    def vector_round(i, device):
        return rcopy(grad, R.grad_in.at[i], sems.ws.at[i], sems.wr.at[i], device)

    def vector_far(i, half, device):
        return rcopy(R.grad_half.at[half], R.grad_far.at[i], sems.ws.at[2 + i], sems.wr.at[2 + i], device)

    first, second = vector_round(0, g.core_peer), vector_round(1, g.y_peer)
    inner = [vector_far(d - 1, 0, g.in_peer(d)) for d in range(1, g.B)]
    outer = [vector_far(g.B + d - 2, 1, g.out_peer(d)) for d in range(1, g.A)]
    first.start()
    part = [qkv_back(R.acc[s], R.sb[s], R.rb[s], R.dq0[s], R.wq0) for s in S]
    first.wait()
    grad[...] += R.grad_in[0]
    second.start()
    step(qp[0])
    qkv_weight(R.wq0, 2 - 2 * g.y, R.x0, R.dq0)
    q0.back_y().start()
    qkv_weight(R.wq0, 1, R.x0, R.dq0)
    q0.send_x(1)
    second.wait()
    grad[...] += R.grad_in[1]
    R.grad_half[0] = grad[...].astype(BF16)
    for x in inner:
        x.start()
    qkv_weight(R.wq0, 2 * g.y, R.x0, R.dq0)
    step(qp[1], op, qp[2], q0, qp[0], o0)
    for s in S:
        part[s].wait()

        def body(i, s=s):
            at = pl.ds(al(i * 16, 16), 16)
            R.dx[s][at, :] = R.ds[s][at, :] + (R.acc[s][at, :] + R.rb[s][at, :].astype(F32))

        tiles(n[s] // 16, body)
    puts = [pltpu.make_async_copy(R.dx[s], out.dx[s], sems.out.at[s]) for s in S]
    for put in puts:
        put.start()
    own_y = [pltpu.make_async_copy(R.yp.at[pl.ds(0, n[s])], out.y[s], sems.out.at[2]) for s in S]
    in_y = [pltpu.make_async_copy(R.yin.at[pl.ds(0, n[s])], out.y[s], sems.out.at[3]) for s in S]

    def put_y(s):
        own_y[s].start()
        y_out[1 - s].wait_recv()
        in_y[1 - s].start()

    for s in S:
        pl.when(this(s))(functools.partial(put_y, s))
    for x in inner:
        x.wait()
    for d in range(1, g.B):
        grad[...] += R.grad_far[d - 1].astype(F32)
    R.grad_half[1] = grad[...].astype(BF16)
    for x in outer:
        x.start()
    step(qp[1], q0, qp[2], o0, q0)
    for x in outer:
        x.wait()
    for d in range(1, g.A):
        grad[...] += R.grad_far[g.B + d - 2].astype(F32)
    final = pltpu.make_async_copy(grad, out.grad, sems.out.at[4])
    final.start()
    last = fp + ip + [op] + qp + [o0, q0]
    while any(done[x.t] < x.stages for x in last):
        for x in last:
            if done[x.t] < x.stages:
                step(x)
    for x in last:
        x.finish()
    for put in puts:
        put.wait()

    def end(s):
        own_y[s].wait()
        in_y[1 - s].wait()
        y_out[s].wait_send()
        dy_give[s].wait_send()

    for s in S:
        pl.when(this(s))(functools.partial(end, s))
    final.wait()
    for d in range(1, g.A):
        vec_z(d).wait_send()
    for d in range(1, g.B):
        for k in range(g.A):
            vec_x(d, k).wait_send()
    for copy in x0_other + key_other:
        copy.wait_send()


def local(
    words,
    regions,
    word_count,
    region_count,
    attn_qkv,
    attn_out,
    attn_bias,
    ffn_in,
    ffn_in_bias,
    ffn_out,
    ffn_out_bias,
    norm_gain,
    norm_bias,
    word_cot,
    region_cot,
    *,
    dp,
    F,
):
    items, nw, D = words.shape
    nr = regions.shape[1]
    FF = ffn_in.shape[2]
    h, hf = D // 2, FF // 2
    A, B = OUTER, F // OUTER
    n = (items * nw, items * nr)
    most = max(n)
    f = lax.axis_index("fsdp")

    small, wide = D // F, FF // F
    lanes = max(window(small, F), window(wide, F))
    at_row = lambda v, row: jnp.pad(v, ((row, VECTORS + 8 - row - v.shape[0]), (0, lanes - v.shape[1])))
    pieces = [attn_bias[0], attn_bias[1], attn_bias[2], ffn_out_bias, norm_gain, norm_bias, ffn_in_bias]
    vectors = sum(at_row(v, row) for v, row in zip(pieces, (0, 3, 6, 9, 11, 16, VECTORS)))

    inputs = dict(
        x=[words.reshape(n[0], D), regions.reshape(n[1], D)],
        live=[word_count, region_count],
        cot=[word_cot.reshape(n[0], D), region_cot.reshape(n[1], D)],
        vectors=vectors,
        attn_qkv=attn_qkv,
        attn_out=attn_out,
        ffn_in=ffn_in,
        ffn_out=ffn_out,
    )
    rs, rf = D // F, FF // F
    rows = VECTORS + 2 * (FF // D)
    shape = jax.ShapeDtypeStruct
    outputs = dict(
        y=[shape((k, D), BF16) for k in n],
        dx=[shape((k, D), F32) for k in n],
        q=shape((3, 3, rs, D), BF16),
        o=shape((3, rs, D), BF16),
        i=shape((2, rs, FF), BF16),
        f=shape((2, rf, D), BF16),
        grad=shape((rows, D), F32),
    )
    dma = pltpu.SemaphoreType.DMA
    slots = A * (B - 1)
    V = lambda *dims: pltpu.VMEM(dims, BF16)
    W = lambda *dims: pltpu.VMEM(dims, F32)

    def shared(total, r, w, *whole):
        return dict(
            y=V(total, w),
            x=[V(slots, r, w) for _ in S],
            z=[V(A - 1, r, w) for _ in S],
            y2=[V(r, w) for _ in S],
            c=V(*whole),
        )

    def private(r, w, half):
        used = slots - A // 2 if half else slots
        return dict(x=[V(1, 8, 128), V(used, r, w)], z=[V(1, 8, 128), V(A - 1, r, w)], fin=V(3, r, w))

    def both(make):
        return [make(k) for k in n]

    T = 10
    scratch = dict(
        wq0=V(3, D, h),
        wo0=V(h, D),
        wq=V(3, D, h),
        wo=V(h, D),
        wi=V(D, hf),
        wf=V(hf, D),
        gq0=shared(D, rs, h, 3, rs, h),
        go0=shared(h, rs, D // 3, rs, D),
        gq=[private(rs, h, False) for _ in range(3)],
        go=private(rs, D, True),
        gi=[private(rs, hf // 2, False) for _ in S],
        gf=[private(rf, D // 2, True) for _ in S],
        vec_in=V(F, VECTORS + 8, lanes),
        vec=W(VECTORS, D + 128),
        vin=W(8, FF + 128),
        grad=W(rows, D),
        grad_in=W(2, rows, D),
        grad_half=V(2, rows, D),
        grad_far=V(B - 1 + A - 1, rows, D),
        keys=W(4, 8, 128 + n[1]),
        masks=W(4, n[0] + n[1], 128 + n[1]),
        x0=both(lambda k: V(2 * k, D)),
        qkv0=both(lambda k: V(3, 2 * k, h)),
        dq0=both(lambda k: V(3, 2 * k, h)),
        c0=both(lambda k: V(2 * k, h)),
        dc0=both(lambda k: V(2 * k, h)),
        p0=[W(HEADS, n[s], n[1 - s]) for s in S],
        acc=both(lambda k: W(k, D)),
        sb=both(lambda k: V(k, D)),
        rb=both(lambda k: V(k, D)),
        xh0=both(lambda k: W(k, D)),
        rr0=both(lambda k: W(k, 128)),
        x1o=both(lambda k: V(k, D)),
        dy=both(lambda k: W(k, D)),
        ds=both(lambda k: W(k, D)),
        f0=both(lambda k: V(2 * k, D)),
        dx=both(lambda k: W(k, D)),
        x1=V(4 * most, D),
        x2=V(4 * most, D),
        qkv=V(3, 4 * most, h),
        dq=V(3, 4 * most, h),
        c=V(4 * most, h),
        dc=V(4 * most, h),
        p=W(2 * HEADS, most, most),
        accp=W(2 * most, D),
        sbp=V(2 * most, D),
        rbp=V(2 * most, D),
        dsp=W(2 * most, D),
        xh=W(2, 2 * most, D),
        rr=W(2, 2 * most, 128),
        f=V(2, 4 * most, D),
        g=V(4 * most, hf),
        gp=V(4 * most, hf),
        du=V(4 * most, hf),
        cot=V(2 * most, D),
        row_live=W(2 * most, 128),
        yp=V(2 * most, D),
        yin=V(most, D),
        dgive=V(most, D),
        dtake=V(most, D),
        sem=dict(
            own=dma((T, 2)),
            zs=dma((T, 2, A - 1)),
            zr=dma((T, 2, A - 1)),
            xs=dma((T, 2, slots)),
            xr=dma((T, 2, slots)),
            ys=dma((T, A)),
            yr=dma((T, A)),
            gys=dma((T,)),
            gyr=dma((T,)),
            gxs=dma((T, 2, slots)),
            gxr=dma((T, 2, slots)),
            gzs=dma((T, 2, A - 1)),
            gzr=dma((T, 2, A - 1)),
            gws=dma((T, 2)),
            gwr=dma((T, 2)),
            gcs=dma((T,)),
            gcr=dma((T,)),
            fs=dma((T, 3)),
            fr=dma((T, 3)),
            put=dma((T, 4)),
            es=dma((48,)),
            er=dma((48,)),
            load=dma((12,)),
            vzs=dma((A - 1,)),
            vzr=dma((A - 1,)),
            vxs=dma((slots,)),
            vxr=dma((slots,)),
            ws=dma((2 + A - 1 + B - 1,)),
            wr=dma((2 + A - 1 + B - 1,)),
            out=dma((5,)),
        ),
    )

    any_spec = pl.BlockSpec(memory_space=pl.ANY)
    leaf = lambda v: not isinstance(v, (dict, list, tuple))
    tree = jax.tree.structure((inputs, outputs, scratch), is_leaf=leaf)
    out_list, out_tree = jax.tree.flatten(outputs, is_leaf=leaf)
    in_list = jax.tree.leaves(inputs, is_leaf=leaf)
    made = pl.pallas_call(
        functools.partial(kernel, tree, (F, D, FF, n, items)),
        out_shape=out_list,
        in_specs=[pl.BlockSpec(memory_space=pltpu.SMEM) if v.ndim == 1 else any_spec for v in in_list],
        out_specs=[any_spec] * len(out_list),
        scratch_shapes=jax.tree.leaves(scratch, is_leaf=leaf),
        compiler_params=pltpu.CompilerParams(
            collective_id=0, has_side_effects=True, vmem_limit_bytes=67_000_000
        ),
        name="layer",
    )(*in_list)
    got = spaces(jax.tree.unflatten(out_tree, made))

    def over_groups(value):
        total = value
        for k in range(1, dp // 4):
            total = total + lax.ppermute(value, "dp", [(r, (r + 4 * k) % dp) for r in range(dp)])
        return total

    weights = [over_groups(v.astype(F32) if dp == 4 else v).astype(F32) for v in (got.q, got.o, got.i, got.f)]
    sums = over_groups(got.grad)
    near = lax.dynamic_slice(sums[:VECTORS], (0, f * small), (VECTORS, small))
    far = lax.dynamic_slice(sums[VECTORS:].reshape(2, FF), (0, f * wide), (2, wide))
    return (
        got.y[0].reshape(words.shape),
        got.y[1].reshape(regions.shape),
        got.dx[0].reshape(words.shape),
        got.dx[1].reshape(regions.shape),
        weights[0],
        weights[1],
        near[:9].reshape(3, 3, small),
        weights[2],
        far,
        weights[3],
        near[9:11],
        near[11:16],
        near[16:21],
    )


def solution(mesh):
    both = ("dp", "fsdp")
    rows = P(both, None, None)
    third, second = P(None, None, "fsdp", None), P(None, "fsdp", None)
    params = (third, second, P(None, None, "fsdp"), second, P(None, "fsdp"), second) + (P(None, "fsdp"),) * 3
    return jax.shard_map(
        functools.partial(local, dp=mesh.shape["dp"], F=mesh.shape["fsdp"]),
        mesh=mesh,
        in_specs=(rows, rows, P(both), P(both)) + params + (rows, rows),
        out_specs=(rows,) * 4 + params,
        check_vma=False,
    )
```

time: 1930 us -> 290 us (0.15)
  waiting for transfers between devices: 1350 us -> 0 us
  Pallas kernels: 0 us -> 267 us
  blocking collectives: 199 us -> 0 us
  local copies, waits for them, and re-layouts: 181 us -> 13.1 us
  matrix products: 120 us -> 0 us
  other arithmetic: 41.4 us -> 8.72 us
    reduce_scatter x7 -> x0, waiting for transfers between devices: 595 us -> none  [the longest x2 199 us: reduce_ffn(): lax.psum_scatter(grads[2].astype(jnp.bfloat16), 'fsdp', scatter_dimension...]
    all_gather x10 -> x0, waiting for transfers between devices: 361 us -> none  [the longest x2 140 us: ffn_params(): lax.all_gather(ffn_out[stream], 'fsdp', axis=0, tiled=True)]
    unnamed x30 -> x0, waiting for transfers between devices: 317 us -> none
    pallas_call x0 -> x1, Pallas kernels: none -> 267 us  [local(): pl.pallas_call(functools.partial(kernel, tree, (F, D, FF, n, items)), out...]
    all_gather x5 -> x0, blocking collectives: 126 us -> none  [the longest x3 80.2 us: attention_params(): lax.all_gather(attn_bias[module], 'fsdp', axis=1, tiled=True)]
    dot_general x60 -> x0, matrix products: 120 us -> none  [product(): return jnp.einsum(pattern, left, right, preferred_element_type=jnp.float32)]
    unnamed x564 -> x26, local copies, waits for them, and re-layouts: 99.2 us -> 5.19 us
    psum x1 -> x0, waiting for transfers between devices: 80.9 us -> none  [reduce_attention(): lax.psum(shards[0].astype(jnp.bfloat16), 'dp').astype(jnp.float32)]
  transfers between devices with their start and end apart: 24 -> 0, of which waited for: 20 -> 0; matrix products, arithmetic and copies ran while one was open for 11% -> 0% of each run, Pallas kernels for 0% -> 0%
where the time goes in v1:
time: 290 us
  Pallas kernels  267 us (92%)
  local copies, waits for them, and re-layouts  13.1 us (5%)
  other arithmetic  8.72 us (3%)
    pallas_call x1, Pallas kernels, local(): pl.pallas_call(functools.partial(kernel, tree, (F, D, FF, n, items)), out...  267 us
    convert_element_type x4, other arithmetic, local(): v.astype(F32)  7.38 us

profile of v1, /device:TPU:1, one launch (start us, length us, event | category | flops | bytes accessed | tf_op | source)
XLA Modules:
  0.0 289.8 jit_solution(4363943922882887073)
XLA Ops:
  0.7 0.8 slice_bitcast_fusion.2
  1.4 1.3 pad_add_fusion.refs_8_
  2.8 1.0 copy.37
  3.7 0.7 reshape.57.refs_3_
  4.5 1.0 copy.39
  5.4 0.7 reshape.59.refs_10_
  6.2 0.7 reshape.56.refs_2_
  6.9 0.7 reshape.58.refs_9_
  7.6 267.2 %layer.1 = (f32[80,768]{1,0:T(8,128)}, f32[144,768]{1,0:T(8,128)}, bf16[2,384,768]{2,1,0:T(8,128)(2,1)}, f32[32,768]{1,0:T(8,128)}, bf16[2,96,3072]{2,1,0:T(8,12...) custom-call(bf16[3,96,768]{2,1,0:T(8,128)(2,1)} %refs_0_.1, ...), custom_call_target="tpu_custom_call" | custom-call | tf_op jit(solution)/shard_map/layer/pallas_call | solution.py:1362
  274.8 0.9 slice.30
  275.7 0.7 fusion
  276.3 0.1 constant_dynamic-slice_fusion
  276.4 0.6 reshape.64
  277.0 0.6 dynamic-slice.1
  277.6 0.7 slice.32
  278.4 0.6 constant_dynamic-slice_fusion.1
  279.0 3.2 %convert_element_type.26 = f32[3,3,96,768]{3,2,1,0:T(8,128)} convert(bf16[3,3,96,768]{3,2,1,0:T(8,128)(2,1)} %get-tuple-element.26) | non-fusion elementwise | flops 663552 | bytes 3981312 | tf_op jit(solution)/shard_map/convert_element_type | solution.py:1381
  282.2 1.7 convert_element_type.28
  283.8 1.6 convert_element_type.29
  285.5 0.9 copy.43
  286.4 1.0 convert_element_type.27
  287.4 0.8 copy.42
  288.3 0.8 copy.41
  289.1 0.7 copy.40
  (25 shorter events, 0.2 us)
Async XLA Ops:
  0.6 5.5 %copy-start.6 = (bf16[4,20,768]{2,0,1:T(4,128)(2,1)S(1)}, bf16[4,20,768]{2,0,1:T(4,128)(2,1)}, u32[]{:S(2)}) copy-start(bf16[4,20,768]{2,0,1:T(4,128)(2,1)} %param.28) | copy-start | bytes 368644
  0.7 6.2 %copy-start.7 = (bf16[4,20,768]{2,0,1:T(4,128)(2,1)S(1)}, bf16[4,20,768]{2,0,1:T(4,128)(2,1)}, u32[]{:S(2)}) copy-start(bf16[4,20,768]{2,0,1:T(4,128)(2,1)} %param.15) | copy-start | bytes 368644
  279.0 3.2 %copy-start.1 = (bf16[2,96,3072]{2,1,0:T(8,128)(2,1)S(1)}, bf16[2,96,3072]{2,1,0:T(8,128)(2,1)}, u32[]{:S(2)}) copy-start(bf16[2,96,3072]{2,1,0:T(8,128)(2,1)} %get-tuple-element.29) | copy-start | bytes 3538948
  282.2 1.7 copy-start
  283.8 1.6 copy-start.2
  285.4 1.0 copy-start.3
  285.5 1.9 copy-start.4
  286.4 1.8 copy-start.5
  287.4 1.7 copy-start.8

commit v2 on v1

--- a/solution.py
+++ b/solution.py
@@ -15,7 +15,7 @@
 NEG = -1e30
 OUTER = 4
 VECTORS = 24
-AHEAD = 3
+AHEAD = 5
 BF16 = jnp.bfloat16
 F32 = jnp.float32
 MESH = pl.DeviceIdType.MESH
@@ -689,6 +689,8 @@
     line[2].start_x()
     for x in line[3:]:
         x.start_z()
+    for x in line[3:AHEAD]:
+        x.start_x()
     cot_own = [load(inp.cot[s], R.cot.at[pl.ds(0, n[s])], False) for s in S]
     cot_other = [exchange(inp.cot[s], R.cot.at[pl.ds(n[s], n[s])], g.y_peer, False) for s in S]
     for s in S:

time: 290 us -> 287 us (0.990)
  Pallas kernels: 267 us -> 264 us
    pallas_call x1, Pallas kernels: 267 us -> 264 us  [local(): pl.pallas_call(functools.partial(kernel, tree, (F, D, FF, n, items)), out...]
where the time goes in v2:
time: 287 us
  Pallas kernels  264 us (92%)
  local copies, waits for them, and re-layouts  13.1 us (5%)
  other arithmetic  8.72 us (3%)
    pallas_call x1, Pallas kernels, local(): pl.pallas_call(functools.partial(kernel, tree, (F, D, FF, n, items)), out...  264 us
    convert_element_type x4, other arithmetic, local(): v.astype(F32)  7.38 us

profile of v2, /device:TPU:1, one launch (start us, length us, event | category | flops | bytes accessed | tf_op | source)
XLA Modules:
  0.0 286.6 jit_solution(1732596412198272426)
XLA Ops:
  0.7 0.8 slice_bitcast_fusion.2
  1.4 1.3 pad_add_fusion.refs_8_
  2.8 1.0 copy.37
  3.7 0.7 reshape.57.refs_3_
  4.5 1.0 copy.39
  5.4 0.7 reshape.59.refs_10_
  6.2 0.7 reshape.56.refs_2_
  6.9 0.7 reshape.58.refs_9_
  7.6 264.0 %layer.1 = (f32[80,768]{1,0:T(8,128)}, f32[144,768]{1,0:T(8,128)}, bf16[2,384,768]{2,1,0:T(8,128)(2,1)}, f32[32,768]{1,0:T(8,128)}, bf16[2,96,3072]{2,1,0:T(8,12...) custom-call(bf16[3,96,768]{2,1,0:T(8,128)(2,1)} %refs_0_.1, ...), custom_call_target="tpu_custom_call" | custom-call | tf_op jit(solution)/shard_map/layer/pallas_call | solution.py:1364
  271.6 0.9 slice.30
  272.5 0.7 fusion
  273.2 0.1 constant_dynamic-slice_fusion
  273.2 0.6 reshape.64
  273.8 0.6 dynamic-slice.1
  274.5 0.7 slice.32
  275.2 0.6 constant_dynamic-slice_fusion.1
  275.8 3.2 %convert_element_type.26 = f32[3,3,96,768]{3,2,1,0:T(8,128)} convert(bf16[3,3,96,768]{3,2,1,0:T(8,128)(2,1)} %get-tuple-element.26) | non-fusion elementwise | flops 663552 | bytes 3981312 | tf_op jit(solution)/shard_map/convert_element_type | solution.py:1383
  279.0 1.7 convert_element_type.28
  280.7 1.6 convert_element_type.29
  282.3 0.9 copy.43
  283.3 1.0 convert_element_type.27
  284.3 0.8 copy.42
  285.1 0.8 copy.41
  285.9 0.7 copy.40
  (25 shorter events, 0.2 us)
Async XLA Ops:
  0.6 5.5 %copy-start.6 = (bf16[4,20,768]{2,0,1:T(4,128)(2,1)S(1)}, bf16[4,20,768]{2,0,1:T(4,128)(2,1)}, u32[]{:S(2)}) copy-start(bf16[4,20,768]{2,0,1:T(4,128)(2,1)} %param.28) | copy-start | bytes 368644
  0.7 6.2 %copy-start.7 = (bf16[4,20,768]{2,0,1:T(4,128)(2,1)S(1)}, bf16[4,20,768]{2,0,1:T(4,128)(2,1)}, u32[]{:S(2)}) copy-start(bf16[4,20,768]{2,0,1:T(4,128)(2,1)} %param.15) | copy-start | bytes 368644
  275.8 3.2 %copy-start.1 = (bf16[2,96,3072]{2,1,0:T(8,128)(2,1)S(1)}, bf16[2,96,3072]{2,1,0:T(8,128)(2,1)}, u32[]{:S(2)}) copy-start(bf16[2,96,3072]{2,1,0:T(8,128)(2,1)} %get-tuple-element.29) | copy-start | bytes 3538948
  279.0 1.7 copy-start
  280.7 1.6 copy-start.2
  282.2 1.0 copy-start.3
  282.3 1.9 copy-start.4
  283.2 1.8 copy-start.5
  284.2 1.7 copy-start.8
